TPU v7x, 32 devices: a whole 2x2x4 slice. The times are simulated.
32 devices in a mesh: dp: 4 (over y, x), ctx: 8 (over z, core).
Axes of the slice: x: 2, y: 2, z: 4, core: 2. Of those that a mesh axis runs over, the one named last changes fastest.
Arguments:
- tokens: bfloat16 [4, 4, 1024, 576], P(None, 'dp', 'ctx'), may hold values from -6 to 6
- prefix: int32 [4, 4], P(None, 'dp'), may hold values from 102 to 512
- norm_attn: bfloat16 [576], P('ctx'), may hold values from 0.5 to 1.5
- w_query: bfloat16 [576, 576], P('dp', 'ctx'), may hold values from -0.25 to 0.25
- w_key: bfloat16 [576, 192], P('dp', 'ctx'), may hold values from -0.25 to 0.25
- w_value: bfloat16 [576, 192], P('dp', 'ctx'), may hold values from -0.25 to 0.25
- w_output: bfloat16 [576, 576], P('dp', 'ctx'), may hold values from -2 to 2
- norm_ffn: bfloat16 [576], P('ctx'), may hold values from 0.5 to 1.5
- w_gate: bfloat16 [576, 1536], P('dp', 'ctx'), may hold values from -0.25 to 0.25
- w_up: bfloat16 [576, 1536], P('dp', 'ctx'), may hold values from -0.25 to 0.25
- w_down: bfloat16 [1536, 576], P('dp', 'ctx'), may hold values from -0.15625 to 0.15625
- cotangent: bfloat16 [4, 4, 1024, 576], P(None, 'dp', 'ctx'), may hold values from -6 to 6
Outputs:
- block_output: bfloat16 [4, 4, 1024, 576], P(None, 'dp', 'ctx')
- input_grad: float32 [4, 4, 1024, 576], P(None, 'dp', 'ctx')
- grad_norm_attn: float32 [576], P('ctx')
- grad_query: float32 [576, 576], P('dp', 'ctx')
- grad_key: float32 [576, 192], P('dp', 'ctx')
- grad_value: float32 [576, 192], P('dp', 'ctx')
- grad_output: float32 [576, 576], P('dp', 'ctx')
- grad_norm_ffn: float32 [576], P('ctx')
- grad_gate: float32 [576, 1536], P('dp', 'ctx')
- grad_up: float32 [576, 1536], P('dp', 'ctx')
- grad_down: float32 [1536, 576], P('dp', 'ctx')
All inputs are finite; a program needn't handle non-finite values.
Results may differ from a plain program's by a relative error of at most 0.03.
Values may be sent and summed in bfloat16 or wider, within the bound.
No kernel may reach another device: no remote copies, remote signals or barrier semaphores. Data moves between devices by JAX's collectives and lax.ppermute only.
A program may use at most 256 MiB of HBM per device.

v0:
```python
import math

import jax
import jax.numpy as jnp
from jax import lax
from jax.experimental import pallas as pl
from jax.experimental.pallas import tpu as pltpu
from jax.sharding import PartitionSpec as P


H = 9
KV = 3
HD = 64
GRP = H // KV
EPSILON = 1e-05
NEGATIVE = -1e30
BF = jnp.bfloat16
F32 = jnp.float32
VMEM_LIMIT = 56 * 1024 * 1024
SMEM_SPEC = pl.BlockSpec(memory_space=pltpu.SMEM)


def dot(a, b, ca=1, cb=0):
    return lax.dot_general(a, b, (((ca,), (cb,)), ((), ())), preferred_element_type=F32)


def call(body, grid, in_specs, out_specs, out_shape, scratch=()):
    return pl.pallas_call(
        body,
        grid=grid,
        in_specs=in_specs,
        out_specs=out_specs,
        out_shape=out_shape,
        scratch_shapes=list(scratch),
        compiler_params=pltpu.CompilerParams(
            dimension_semantics=("arbitrary",) * len(grid), vmem_limit_bytes=VMEM_LIMIT
        ),
    )


def whole(shape):
    zeros = (0,) * len(shape)
    return pl.BlockSpec(shape, lambda *_: zeros)


def sds(shape, dtype):
    return jax.ShapeDtypeStruct(shape, dtype)


def norm_rows(h):
    return lax.rsqrt(jnp.mean(h * h, -1, keepdims=True) + EPSILON)


def half_swap(x, lane):
    return jnp.where(lane % HD < HD // 2, pltpu.roll(x, 96, 1), pltpu.roll(x, 32, 1))


def place_rows(coords, piece_refs, target_ref):
    slots = len(piece_refs)
    block = piece_refs[0].shape[1]
    for d in range(slots):
        start = pl.multiple_of(lax.rem(coords[1] - d + slots, slots) * block, block)
        value = piece_refs[d][...].astype(F32).T
        target_ref[pl.ds(start, block), :] = value.astype(target_ref.dtype)


def pick_rows(coords, source_ref, piece_refs):
    slots = len(piece_refs)
    block = piece_refs[0].shape[1]
    for d in range(slots):
        start = pl.multiple_of(lax.rem(coords[1] + d, slots) * block, block)
        value = source_ref[pl.ds(start, block), :].T
        piece_refs[d][...] = value.astype(piece_refs[d].dtype)


def qkv_forward(h, gain, w, cs, sn, coords=None):
    dealt = coords is not None
    pieces = list(h) if dealt else [h]
    width, rows = w.shape[0], cs.shape[0]

    def body(*refs):
        if dealt:
            co, *piece_refs = refs[: 1 + len(pieces)]
            refs = refs[1 + len(pieces) :]
            h_ref = refs[-1]
            place_rows(co, piece_refs, h_ref)
        else:
            h_ref, *refs = refs
        g_ref, w_ref, cs_ref, sn_ref, na_ref, q_ref, kv_ref = refs[:7]
        x = h_ref[...]
        na = (x * norm_rows(x) * g_ref[0:1, :]).astype(BF)
        na_ref[...] = na
        y = dot(na, w_ref[...])
        lane = lax.broadcasted_iota(jnp.int32, (rows, 128), 1)
        low = lane < HD
        cosine = cs_ref[...]
        sine = sn_ref[...]
        turned = []
        for c in range((H + KV) // 2):
            x = y[:, 128 * c : 128 * c + 128]
            turned.append(x * cosine + half_swap(x, lane) * sine)
        for head in range(H):
            x = turned[head // 2] * (HD**-0.5)
            if head % 2:
                x = pltpu.roll(x, 64, 1)
            q_ref[head] = jnp.where(low, x, 0.0).astype(BF)
        base = (H + KV) * HD
        for j in range(KV):
            k = turned[(H + j) // 2]
            if (H + j) % 2:
                k = pltpu.roll(k, 64, 1)
            v = y[:, base + HD * j : base + HD * j + HD]
            kv_ref[j] = jnp.concatenate([k[:, :HD], v], axis=1).astype(BF)

    return call(
        body,
        (1,),
        ([SMEM_SPEC] if dealt else [])
        + [whole(x.shape) for x in pieces + [gain, w, cs, sn]],
        [whole((rows, width)), whole((H, rows, 128)), whole((KV, rows, 128))]
        + ([whole((rows, width))] if dealt else []),
        [sds((rows, width), BF), sds((H, rows, 128), BF), sds((KV, rows, 128), BF)]
        + ([sds((rows, width), F32)] if dealt else []),
    )(*([coords] if dealt else []), *pieces, gain, w, cs, sn)


def key_bounds(slots, parts):
    return [max(parts * (s + 1), parts * slots // 2) for s in range(slots)]


def gather_keys(kv_refs, full_ref, slots, block):
    parts = len(kv_refs)
    for t in range(slots):
        for e in range(parts):
            start = (parts * t + e) * block
            full_ref[start : start + block, :] = kv_refs[e][0, t * block : t * block + block, :]


def attend_forward(q, kv_parts, meta, slots):
    parts = len(kv_parts)
    rows = q.shape[1]
    block = rows // slots
    bounds = key_bounds(slots, parts)

    def body(meta_ref, q_ref, *refs):
        kv_refs = refs[:parts]
        att_ref, linv_ref = refs[parts : parts + 2]
        p_refs = refs[parts + 2 : parts + 2 + slots]
        full_ref, turned_ref = refs[-2:]
        gather_keys(kv_refs, full_ref, slots, block)
        turned_ref[...] = full_ref[...].T
        prefix = meta_ref[0]
        lane = lax.broadcasted_iota(jnp.int32, (block, 128), 1)
        for s in range(slots):
            free = parts * s * block
            top = bounds[s] * block
            q_pos = (parts * s + meta_ref[1]) * block + lax.broadcasted_iota(
                jnp.int32, (block, block), 1
            )
            key_iota = lax.broadcasted_iota(jnp.int32, (block, block), 0)
            biases = []
            for t in range(s, bounds[s] // parts):
                for e in range(parts):
                    k_pos = (parts * t + meta_ref[1 + e]) * block + key_iota
                    biases.append(
                        jnp.where((k_pos <= q_pos) | (k_pos < prefix), 0.0, NEGATIVE)
                    )
            bias = jnp.concatenate(biases, axis=0)
            bias = jnp.concatenate([bias] * GRP, axis=1)
            here = slice(s * block, s * block + block)
            qs = q_ref[:, here, :].reshape(GRP * block, 128)
            masked = dot(full_ref[free:top, :], qs, 1, 1) + bias
            top_score = jnp.max(masked, 0, keepdims=True)
            if free:
                opened = dot(full_ref[:free, :], qs, 1, 1)
                top_score = jnp.maximum(top_score, jnp.max(opened, 0, keepdims=True))
            term = jnp.exp(masked - top_score)
            total = jnp.sum(term, 0, keepdims=True)
            pb = term.astype(BF)
            p_refs[s][0, free:top, :] = pb
            mix = dot(turned_ref[:, free:top], pb)
            if free:
                term = jnp.exp(opened - top_score)
                total = total + jnp.sum(term, 0, keepdims=True)
                pb = term.astype(BF)
                p_refs[s][0, :free, :] = pb
                mix = mix + dot(turned_ref[:, :free], pb)
            inverse = 1.0 / total
            sub = lax.broadcasted_iota(jnp.int32, (128, GRP * block), 0)
            mix = jnp.where(sub == 0, inverse, mix * inverse).T
            outs = [mix[hh * block : hh * block + block, HD:].astype(BF) for hh in range(GRP)]
            linvs = [mix[hh * block : hh * block + block, 0:1] for hh in range(GRP)]
            att_ref[0, s * block : s * block + block, :] = jnp.concatenate(outs, axis=1)
            packed = jnp.where(lane == 0, linvs[0], jnp.where(lane == 1, linvs[1], linvs[2]))
            linv_ref[0, s * block : s * block + block, :] = packed

    def head_block(shape):
        return pl.BlockSpec((1,) + shape, lambda j: (j,) + (0,) * len(shape))

    return call(
        body,
        (KV,),
        [
            pl.BlockSpec(memory_space=pltpu.SMEM),
            pl.BlockSpec((GRP, rows, 128), lambda j: (j, 0, 0)),
        ]
        + [head_block((rows, 128))] * parts,
        [head_block((rows, GRP * HD)), head_block((rows, 128))]
        + [head_block((b * block, GRP * block)) for b in bounds],
        [sds((KV, rows, GRP * HD), BF), sds((KV, rows, 128), F32)]
        + [sds((KV, b * block, GRP * block), BF) for b in bounds],
        [pltpu.VMEM((parts * rows, 128), BF), pltpu.VMEM((128, parts * rows), BF)],
    )(meta, q, *kv_parts)


def attend_backward(q, kv_parts, datt, att, linv, probs, cs, sn, slots, first=0, count=KV):
    parts = len(kv_parts)
    rows = q.shape[1]
    block = rows // slots
    bounds = key_bounds(slots, parts)
    total_keys = parts * rows

    def body(q_ref, datt_ref, att_ref, linv_ref, cs_ref, sn_ref, *refs):
        kv_refs = refs[:parts]
        p_refs = refs[parts : parts + slots]
        dq_ref = refs[parts + slots]
        dkv_refs = refs[parts + slots + 1 : parts + slots + 1 + parts]
        full_ref, turned_ref, acc_ref = refs[-3:]
        gather_keys(kv_refs, full_ref, slots, block)
        keys = full_ref[...]
        turned_ref[...] = keys.T
        key_lane = lax.broadcasted_iota(jnp.int32, keys.shape, 1)
        ones = jnp.where(key_lane < 2, 1.0, 0.0)
        full_ref[...] = jnp.where(key_lane < HD, ones, keys.astype(F32)).astype(BF)
        acc_ref[...] = jnp.zeros_like(acc_ref)
        lane = lax.broadcasted_iota(jnp.int32, (block, 128), 1)
        for s in range(slots):
            top = bounds[s] * block
            here = slice(s * block, s * block + block)
            d_all = datt_ref[0, here, :].astype(F32)
            product = d_all * att_ref[0, here, :].astype(F32)
            plain = []
            shifts = []
            for hh in range(GRP):
                inverse = linv_ref[0, here, hh : hh + 1]
                cols = slice(hh * HD, hh * HD + HD)
                delta = jnp.sum(product[:, cols], -1, keepdims=True) * inverse
                scaled = jnp.concatenate(
                    [jnp.zeros((block, HD), F32), d_all[:, cols] * inverse], axis=1
                )
                coarse = delta.astype(BF).astype(F32)
                fine = jnp.where(lane == 1, coarse - delta, 0.0)
                plain.append(scaled.astype(BF))
                shifts.append((scaled + jnp.where(lane == 0, -coarse, fine)).astype(BF))
            plain = jnp.concatenate(plain, axis=0)
            shifts = jnp.concatenate(shifts, axis=0)
            dp = dot(full_ref[:top, :], shifts, 1, 1)
            pb = p_refs[s][0]
            ds = (pb.astype(F32) * dp).astype(BF)
            dq = dot(turned_ref[:, :top], ds).T
            dqs = [dq[hh * block : hh * block + block] for hh in range(GRP)]
            qs = q_ref[:, here, :].reshape(GRP * block, 128)
            acc_ref[:top, :] += dot(
                jnp.concatenate([ds, pb], axis=1), jnp.concatenate([qs, plain], axis=0)
            )
            cosine = cs_ref[here, :]
            sine = sn_ref[here, :]
            outs = []
            for x in dqs:
                x = x * (HD**-0.5)
                x = x * cosine - half_swap(x, lane) * sine
                outs.append(x[:, :HD].astype(BF))
            dq_ref[0, here, :] = jnp.concatenate(outs, axis=1)
        for t in range(slots):
            for e in range(parts):
                start = (parts * t + e) * block
                dkv_refs[e][0, t * block : t * block + block, :] = acc_ref[
                    start : start + block, :
                ].astype(BF)

    def head_block(shape, start=first):
        return pl.BlockSpec((1,) + shape, lambda j: (j + start,) + (0,) * len(shape))

    return call(
        body,
        (count,),
        [
            pl.BlockSpec((GRP, rows, 128), lambda j: (j + first, 0, 0)),
            head_block((rows, GRP * HD)),
            head_block((rows, GRP * HD)),
            head_block((rows, 128)),
            whole(cs.shape),
            whole(sn.shape),
        ]
        + [head_block((rows, 128))] * parts
        + [head_block((b * block, GRP * block)) for b in bounds],
        [head_block((rows, GRP * HD), 0)] + [head_block((rows, 128), 0)] * parts,
        [sds((count, rows, GRP * HD), BF)] + [sds((count, rows, 128), BF)] * parts,
        [
            pltpu.VMEM((total_keys, 128), BF),
            pltpu.VMEM((128, total_keys), BF),
            pltpu.VMEM((total_keys, 128), F32),
        ],
    )(q, datt, att, linv, cs, sn, *kv_parts, *probs)


def ffn_forward(h, att, w_out, gain, w_gate, w_up, w_down, coords=None, slots=4, width_f=512):
    rows, width = h.shape
    ff = w_gate.shape[1]
    steps = ff // width_f
    last = coords is not None

    def body(*refs):
        if last:
            co, *refs = refs
        h_ref, att_ref, wo_ref, g_ref, wg_ref, wu_ref, wd_ref = refs[:7]
        refs = refs[7:]
        h1_ref, nb_ref, a_ref, b_ref, hid_ref, h2_ref = refs[:6]
        f = pl.program_id(0)

        @pl.when(f == 0)
        def _():
            h1 = h_ref[...].astype(F32)
            for j in range(KV):
                h1 = h1 + dot(att_ref[j], wo_ref[GRP * HD * j : GRP * HD * (j + 1), :])
            h1_ref[...] = h1
            h2_ref[...] = h1
            nb_ref[...] = (h1 * norm_rows(h1) * g_ref[1:2, :]).astype(BF)

        nb = nb_ref[...]
        gate = dot(nb, wg_ref[...])
        up = dot(nb, wu_ref[...])
        sig = 1.0 / (1.0 + jnp.exp(-gate))
        silu = gate * sig
        hid = (silu * up).astype(BF)
        hid_ref[...] = hid
        b_ref[...] = silu.astype(BF)
        a_ref[...] = (up * (sig + silu * (1.0 - sig))).astype(BF)
        h2_ref[...] += dot(hid, wd_ref[...], 1, 1)
        if last:

            @pl.when(f == steps - 1)
            def _():
                pick_rows(co, h2_ref, refs[6:])

    tall = pl.BlockSpec((width, width_f), lambda f: (0, f))
    acts = pl.BlockSpec((rows, width_f), lambda f: (0, f))
    out_specs = [whole((rows, width)), whole((rows, width)), acts, acts, acts, whole((rows, width))]
    out_shape = [
        sds((rows, width), F32),
        sds((rows, width), BF),
        sds((rows, ff), BF),
        sds((rows, ff), BF),
        sds((rows, ff), BF),
        sds((rows, width), F32),
    ]
    if last:
        out_specs += [whole((width, rows // slots))] * slots
        out_shape += [sds((width, rows // slots), BF)] * slots
    return call(
        body,
        (steps,),
        ([SMEM_SPEC] if last else [])
        + [
            whole(h.shape),
            whole(att.shape),
            whole(w_out.shape),
            whole(gain.shape),
            tall,
            tall,
            tall,
        ],
        out_specs,
        out_shape,
    )(*([coords] if last else []), h, att, w_out, gain, w_gate, w_up, w_down)


def ffn_backward(g, kept, full, previous, coords=None, width_f=512):
    h1, nb, a, b, hid, att = kept
    w_out, gain, w_gate, w_up, w_down = full
    rows, width = h1.shape
    ff = w_gate.shape[1]
    steps = ff // width_f
    final = previous is not None
    kind = BF if final else F32
    dealt = coords is not None
    streams = list(g) if dealt else [g]

    def body(*refs):
        if dealt:
            co, *refs = refs
        g_refs, refs = refs[: len(streams)], refs[len(streams) - 1 :]
        a_ref, b_ref, hid_ref, nb_ref, h1_ref, att_ref = refs[1:7]
        gain_ref, wo_ref, wg_ref, wu_ref, wd_ref = refs[7:12]
        refs = refs[12:]
        if final:
            pd_ref, pg_ref, pu_ref, po_ref, pn_ref = refs[:5]
            refs = refs[5:]
        gd_ref, gg_ref, gu_ref, go_ref, gn_ref, g1_ref, datt_ref = refs[:7]
        nbt_ref, e2_ref, e2t_ref, dnb_ref = refs[7:]
        f = pl.program_id(0)

        @pl.when(f == 0)
        def _():
            nbt_ref[...] = nb_ref[...].T
            if dealt:
                place_rows(co, g_refs, e2_ref)
            else:
                e2_ref[...] = g_refs[0][...].astype(BF)
            e2t_ref[...] = e2_ref[...].T
            dnb_ref[...] = jnp.zeros_like(dnb_ref)

        e2 = e2_ref[...]
        dh = dot(e2, wd_ref[...])
        dgate = (dh * a_ref[...].astype(F32)).astype(BF)
        dup = (dh * b_ref[...].astype(F32)).astype(BF)
        dnb_ref[...] += dot(dgate, wg_ref[...], 1, 1) + dot(dup, wu_ref[...], 1, 1)
        nbt = nbt_ref[...]
        gd = dot(e2t_ref[...], hid_ref[...])
        gg = dot(nbt, dgate)
        gu = dot(nbt, dup)
        if final:
            gd = gd + pd_ref[...]
            gg = gg + pg_ref[...]
            gu = gu + pu_ref[...]
        gd_ref[...] = gd.astype(kind)
        gg_ref[...] = gg.astype(kind)
        gu_ref[...] = gu.astype(kind)

        @pl.when(f == steps - 1)
        def _():
            h1v = h1_ref[...]
            r = norm_rows(h1v)
            dnb = dnb_ref[...]
            gn = jnp.sum(dnb * h1v * r, 0, keepdims=True)
            u = dnb * gain_ref[1:2, :]
            g1 = (
                (e2_ref if dealt else g_refs[0])[...].astype(F32)
                + r * u
                - h1v * (r * r * r * jnp.mean(u * h1v, -1, keepdims=True))
            )
            g1_ref[...] = g1
            e1 = g1.astype(BF)
            for j in range(KV):
                span = slice(GRP * HD * j, GRP * HD * (j + 1))
                datt_ref[j] = dot(e1, wo_ref[span, :], 1, 1).astype(BF)
                go = dot(att_ref[j], e1, 0, 0)
                if final:
                    go = go + po_ref[span, :]
                go_ref[span, :] = go.astype(kind)
            if final:
                gn = gn + pn_ref[...]
            gn_ref[...] = gn

    tall = pl.BlockSpec((width, width_f), lambda f: (0, f))
    acts = pl.BlockSpec((rows, width_f), lambda f: (0, f))
    one = whole((1, width))
    grads = [tall, tall, tall, whole((width, width)), one]
    return call(
        body,
        (steps,),
        ([SMEM_SPEC] if dealt else [])
        + [whole(x.shape) for x in streams]
        + [acts, acts, acts, whole(nb.shape), whole(h1.shape), whole(att.shape)]
        + [whole(gain.shape), whole(w_out.shape), tall, tall, tall]
        + (grads if final else []),
        grads + [whole((rows, width)), whole((KV, rows, GRP * HD))],
        [
            sds((width, ff), kind),
            sds((width, ff), kind),
            sds((width, ff), kind),
            sds((width, width), kind),
            sds((1, width), F32),
            sds((rows, width), F32),
            sds((KV, rows, GRP * HD), BF),
        ],
        [
            pltpu.VMEM((width, rows), BF),
            pltpu.VMEM((rows, width), BF),
            pltpu.VMEM((width, rows), BF),
            pltpu.VMEM((rows, width), F32),
        ],
    )(
        *([coords] if dealt else []),
        *streams,
        *(a, b, hid, nb, h1, att, gain, w_out, w_gate, w_up, w_down),
        *(previous or ()),
    )


def qkv_backward(dq, dkv, na, h, g1, gain, w, cs, sn, before, coords=None, slots=4):
    rows, width = na.shape
    pieces = len(dq)
    cols = w.shape[1]
    final = coords is not None

    def body(*refs):
        if final:
            co, *refs = refs
        dq_refs, refs = refs[:pieces], refs[pieces:]
        dkv_refs, refs = refs[: len(dkv)], refs[len(dkv) :]
        na_ref, h_ref, g1_ref, gain_ref, w_ref, cs_ref, sn_ref = refs[:7]
        refs = refs[7:]
        if final:
            pn_ref, d_ref, gn_ref, *piece_refs, g0_ref = refs
        else:
            gw_ref, gn_ref, g0_ref = refs
        lane = lax.broadcasted_iota(jnp.int32, (rows, 128), 1)
        cosine = cs_ref[...]
        sine = sn_ref[...]
        ks = []
        vs = []
        for j in range(KV):
            where = [(n, k) for n in range(pieces) for k in range(dq[n].shape[0])][j]
            mine = dkv_refs[where[0] :: pieces]
            x = mine[0][where[1]].astype(F32)
            for ref in mine[1:]:
                x = x + ref[where[1]].astype(F32)
            k = x * cosine - half_swap(x, lane) * sine
            ks.append(k[:, :HD].astype(BF))
            vs.append(x[:, HD:].astype(BF))
        qs = [ref[k] for ref in dq_refs for k in range(ref.shape[0])]
        d = jnp.concatenate(qs + ks + vs, axis=1)
        dna = dot(d, w_ref[...], 1, 1)
        if final:
            d_ref[...] = d
        else:
            gw_ref[...] = dot(na_ref[...], d, 0, 0)
        x = h_ref[...].astype(F32)
        r = norm_rows(x)
        gn = jnp.sum(dna * x * r, 0, keepdims=True)
        u = dna * gain_ref[0:1, :]
        g0_ref[...] = (
            g1_ref[...] + r * u - x * (r * r * r * jnp.mean(u * x, -1, keepdims=True))
        )
        if final:
            gn = gn + pn_ref[...]
            pick_rows(co, g0_ref, piece_refs)
        gn_ref[...] = gn

    args = [*dq, *dkv, na, h, g1, gain, w, cs, sn] + ([before] if final else [])
    shapes = [((1, width), F32)]
    if final:
        shapes = [((rows, cols), BF)] + shapes + [((width, rows // slots), BF)] * slots
    else:
        shapes = [((width, cols), F32)] + shapes + [((rows, width), F32)]
    return call(
        body,
        (1,),
        ([SMEM_SPEC] if final else []) + [whole(x.shape) for x in args],
        [whole(x) for x, _ in shapes],
        [sds(x, t) for x, t in shapes],
        [pltpu.VMEM((rows, width), F32)] if final else [],
    )(*([coords] if final else []), *args)


def qkv_weights(d, na, before):
    def body(d_ref, na_ref, pw_ref, gw_ref):
        gw_ref[...] = (dot(na_ref[...], d_ref[...], 0, 0) + pw_ref[...]).astype(BF)

    args = (d, na, before)
    return call(
        body, (1,), [whole(x.shape) for x in args], [whole(before.shape)], [sds(before.shape, BF)]
    )(*args)[0]


def shifted(total, group, step):
    pairs = []
    for i in range(total):
        z, c = divmod(i, group)
        pairs.append((i, ((z + step) % (total // group)) * group + c))
    return pairs


def within(total, group, step):
    return [(i, (i // group) * group + (i % group + step) % group) for i in range(total)]


WQ = H * HD
WK = KV * HD
COLS_A = (0, 72, 96, 120)
FOLDS = ((0, 32), (32, 32), (64, 32), (96, 32), (128, 16))
ROWS_D = 144
ROWS_F = 256
TOP = ROWS_D


def fold_out(out, cols):
    parts = []
    for start, count in FOLDS:
        part = out[start : start + count, cols]
        if count < 32:
            part = jnp.concatenate([part, jnp.zeros((32 - count, 72), part.dtype)], axis=0)
        parts.append(part)
    return jnp.concatenate(parts + [jnp.zeros((32, 24), out.dtype)], axis=1)


def pack_shards(shards):
    def body(wq, wk, wv, wo, wg, wu, wd, ga, gf, a_ref, top_ref, low_ref):
        wk_rows, wv_rows = [ref[...].astype(F32).T.astype(BF) for ref in (wk, wv)]
        a_ref[:ROWS_D, :] = jnp.concatenate(
            [wq[...], wk_rows, wv_rows, jnp.zeros((ROWS_D, 8), BF)], axis=1
        )
        row = lax.broadcasted_iota(jnp.int32, (16, 72), 0)
        ga_row = ga[...].astype(F32)
        gf_row = gf[...].astype(F32)
        gains = jnp.where(row == 0, ga_row, jnp.where(row == 1, gf_row, 0.0))
        a_ref[ROWS_D:, :] = jnp.concatenate([gains, jnp.zeros((16, 56), F32)], axis=1).astype(BF)
        wide = jnp.concatenate(
            [wg[:, :128], wu[:, :128], wg[:, 128:], wu[:, 128:]], axis=1
        )
        top_ref[...] = wide
        low_ref[:32, :] = fold_out(wo[...], slice(0, 72))
        down = jnp.concatenate(
            [wd[:, :128], wd[:, 192:320], wd[:, 128:192], wd[:, 320:]], axis=1
        ).astype(F32)
        low_ref[32:, :] = jnp.concatenate([down, jnp.zeros((8, 384), F32)], axis=0).astype(BF)

    return call(
        body,
        (1,),
        [whole(x.shape) for x in shards],
        [whole((160, 128)), whole((TOP, 384)), whole((ROWS_F - TOP, 384))],
        [sds((160, 128), BF), sds((TOP, 384), BF), sds((ROWS_F - TOP, 384), BF)],
    )(*shards)


def cross(step, count):
    return [(i, i ^ step) for i in range(count)]


def spread_z(x):
    return [x] + [lax.ppermute(x, "ctx", shifted(8, 2, d)) for d in (1, 2, 3)]


def spread_attn(pieces, mark):
    stack = jnp.stack(pieces)
    mine = [lax.ppermute(stack, "dp", cross(r, 4)) for r in (1, 2, 3)]
    mine = [stack] + after(mine, mark)
    return mine + [lax.ppermute(m, "ctx", cross(1, 8)) for m in mine]


def spread_ffn(top, low):
    top, low = jnp.stack(top), jnp.stack(low)
    top_x = lax.ppermute(top, "dp", cross(1, 4))
    low_y = lax.ppermute(low, "dp", cross(2, 4))
    top_y = lax.ppermute(top, "dp", cross(2, 4))
    low_x = lax.ppermute(low, "dp", cross(1, 4))
    top_far = lax.ppermute(top_x, "dp", cross(2, 4))
    low_far = lax.ppermute(low_y, "dp", cross(1, 4))
    mine = [top, top_x, top_y, top_far, low, low_x, low_y, low_far]
    return mine + [lax.ppermute(m, "ctx", cross(1, 8)) for m in mine]


def ordered(c, own, sibling):
    return jnp.where(c == 0, own, sibling), jnp.where(c == 0, sibling, own)


def assemble_attn(coords, arrays):
    def body(co, *refs):
        own, sib = refs[:4], refs[4:8]
        w_ref, g_ref = refs[8:]
        j_own, z_own, c_own = co[0], co[1], co[2]
        for r in range(4):
            row = pl.multiple_of((j_own ^ r) * ROWS_D, 16)
            pieces = []
            for z in range(4):
                d = lax.rem(z_own - z + 4, 4)
                pieces.extend(ordered(c_own, own[r][d], sib[r][d]))
            groups = [
                jnp.concatenate([p[:ROWS_D, a:b] for p in pieces], axis=1)
                for a, b in zip(COLS_A[:-1], COLS_A[1:])
            ]
            w_ref[pl.ds(row, ROWS_D), :] = jnp.concatenate(groups, axis=1)
            if r == 0:
                g_ref[...] = jnp.concatenate(
                    [p[ROWS_D:, :72].astype(F32) for p in pieces], axis=1
                )

    shapes = [((576, 960), BF), ((16, 576), F32)]
    return call(
        body,
        (1,),
        [SMEM_SPEC] + [whole(x.shape) for x in arrays],
        [whole(s) for s, _ in shapes],
        [sds(s, t) for s, t in shapes],
    )(coords, *arrays)


def assemble_ffn(coords, arrays):
    def body(co, *refs):
        own, sib = refs[:8], refs[8:16]
        o_ref, g_ref, u_ref, d_ref = refs[16:]
        j_own, z_own, c_own = co[0], co[1], co[2]

        def read(group, r, d):
            return jnp.concatenate([group[r][d], group[4 + r][d]], axis=0)

        for r in range(4):
            j = j_own ^ r
            row = pl.multiple_of(j * ROWS_D, 16)
            lane = pl.multiple_of(j * 384, 128)
            pieces = []
            for z in range(4):
                d = lax.rem(z_own - z + 4, 4)
                even, odd = ordered(c_own, read(own, r, d), read(sib, r, d))
                pieces.extend((even, odd))
                here = slice(384 * z, 384 * z + 384)
                for ref, first, rest in ((g_ref, 0, 256), (u_ref, 128, 320)):
                    ref[pl.ds(row, ROWS_D), here] = jnp.concatenate(
                        [
                            even[:ROWS_D, first : first + 128],
                            odd[:ROWS_D, first : first + 128],
                            even[:ROWS_D, rest : rest + 64],
                            odd[:ROWS_D, rest : rest + 64],
                        ],
                        axis=1,
                    )
                down = jnp.concatenate(
                    [even[176:248].astype(F32), odd[176:248].astype(F32)], axis=0
                )
                d_ref[ROWS_D * z : ROWS_D * z + ROWS_D, pl.ds(lane, 384)] = down.astype(BF)
            for g, (start, count) in enumerate(FOLDS):
                o_ref[pl.ds(pl.multiple_of(row + start, 16), count), :] = jnp.concatenate(
                    [p[144 : 144 + count, 72 * g : 72 * g + 72] for p in pieces], axis=1
                )

    shapes = [(576, 576), (576, 1536), (576, 1536), (576, 1536)]
    return call(
        body,
        (1,),
        [SMEM_SPEC] + [whole(x.shape) for x in arrays],
        [whole(s) for s in shapes],
        [sds(s, BF) for s in shapes],
    )(coords, *arrays)


def split_attn(coords, d_qkv, na, before, gn_attn, gn_ffn):
    def body(co, d_ref, na_ref, pw_ref, ga, gf, *outs):
        keep, away, gw = outs[:4], outs[4], outs[5]
        gw[...] = (dot(na_ref[...], d_ref[...], 0, 0) + pw_ref[...]).astype(BF)
        j_own, z_own, c_own = co[0], co[1], co[2]
        sub = lax.broadcasted_iota(jnp.int32, (16, 576), 0)
        gains = jnp.where(sub == 0, ga[...], jnp.where(sub == 1, gf[...], 0.0)).astype(BF)
        for r in range(4):
            row = pl.multiple_of((j_own ^ r) * ROWS_D, 16)
            wide = gw[pl.ds(row, ROWS_D), :]
            for z in range(4):
                d = lax.rem(z - z_own + 4, 4)
                pair = []
                for k in (2 * z, 2 * z + 1):
                    top = jnp.concatenate(
                        [
                            wide[:, 72 * k : 72 * k + 72],
                            wide[:, WQ + 24 * k : WQ + 24 * k + 24],
                            wide[:, WQ + WK + 24 * k : WQ + WK + 24 * k + 24],
                            jnp.zeros((ROWS_D, 8), BF),
                        ],
                        axis=1,
                    )
                    low = jnp.concatenate(
                        [gains[:, 72 * k : 72 * k + 72], jnp.zeros((16, 56), BF)], axis=1
                    )
                    pair.append(jnp.concatenate([top, low], axis=0))
                mine, other = ordered(c_own, *pair)
                keep[r][d] = mine
                away[r, d] = other

    shapes = [(4, 160, 128)] * 4 + [(4, 4, 160, 128)]
    args = (d_qkv, na, before, gn_attn, gn_ffn)
    return call(
        body,
        (1,),
        [SMEM_SPEC] + [whole(x.shape) for x in args],
        [whole(s) for s in shapes],
        [sds(s, BF) for s in shapes],
        [pltpu.VMEM(before.shape, BF)],
    )(coords, *args)


def split_ffn(coords, g_out, g_gate, g_up, g_down):
    def body(co, go, gg, gu, gd, *outs):
        keep, away = outs[:4], outs[4]
        j_own, z_own, c_own = co[0], co[1], co[2]
        for r in range(4):
            j = j_own ^ r
            row = pl.multiple_of(j * ROWS_D, 16)
            lane = pl.multiple_of(j * 384, 128)
            out = go[pl.ds(row, ROWS_D), :]
            for z in range(4):
                d = lax.rem(z - z_own + 4, 4)
                gate = gg[pl.ds(row, ROWS_D), 384 * z : 384 * z + 384]
                up = gu[pl.ds(row, ROWS_D), 384 * z : 384 * z + 384]
                down = gd[ROWS_D * z : ROWS_D * z + ROWS_D, pl.ds(lane, 384)].astype(F32)
                pair = []
                for i in range(2):
                    k = 2 * z + i
                    first = slice(128 * i, 128 * i + 128)
                    rest = slice(256 + 64 * i, 320 + 64 * i)
                    wide = jnp.concatenate(
                        [gate[:, first], up[:, first], gate[:, rest], up[:, rest]], axis=1
                    )
                    low = jnp.concatenate(
                        [down[72 * i : 72 * i + 72], jnp.zeros((8, 384), F32)], axis=0
                    ).astype(BF)
                    pair.append((wide, fold_out(out, slice(72 * k, 72 * k + 72)), low))
                spans = (slice(0, 144), slice(144, 176), slice(176, 256))
                for part, here in enumerate(spans):
                    mine, other = ordered(c_own, pair[0][part], pair[1][part])
                    keep[r][d, here, :] = mine
                    away[r, d, here, :] = other

    shapes = [(4, ROWS_F, 384)] * 4 + [(4, 4, ROWS_F, 384)]
    args = (g_out, g_gate, g_up, g_down)
    return call(
        body,
        (1,),
        [SMEM_SPEC] + [whole(x.shape) for x in args],
        [whole(s) for s in shapes],
        [sds(s, BF) for s in shapes],
    )(coords, *args)


def total(*terms):
    out = terms[0].astype(F32)
    for t in terms[1:]:
        out = out + t.astype(F32)
    return out.astype(BF)


def sum_z(mine):
    return [mine[0]] + [lax.ppermute(mine[d], "ctx", shifted(8, 2, d)) for d in (1, 2, 3)]


def sum_attn(pieces):
    keep, away = pieces[:4], pieces[4]
    back = lax.ppermute(away, "ctx", cross(1, 8))
    moved = [lax.ppermute(total(keep[r], back[r]), "dp", cross(r, 4)) for r in (1, 2, 3)]
    return sum_z(total(keep[0], back[0], *moved))


def sum_ffn(pieces):
    keep, away = pieces[:4], pieces[4]
    back = lax.ppermute(away, "ctx", cross(1, 8))
    top, low = slice(0, TOP), slice(TOP, ROWS_F)

    def pair(r, rows, *more):
        return total(keep[r][:, rows], back[r][:, rows], *more)

    far_top, far_low = pair(3, top), pair(3, low)
    x_low, y_top = pair(1, low), pair(2, top)
    top_far = lax.ppermute(far_top, "dp", cross(2, 4))
    low_far = lax.ppermute(far_low, "dp", cross(1, 4))
    low_x = lax.ppermute(x_low, "dp", cross(1, 4))
    top_y = lax.ppermute(y_top, "dp", cross(2, 4))
    x_top, y_low = pair(1, top, top_far), pair(2, low, low_far)
    top_x = lax.ppermute(x_top, "dp", cross(1, 4))
    low_y = lax.ppermute(y_low, "dp", cross(2, 4))
    mine = jnp.concatenate([pair(0, top, top_x, top_y), pair(0, low, low_x, low_y)], axis=1)
    return sum_z(mine), (away, (far_top, far_low, x_low, y_top))


def finish(terms_f, terms_a):
    def body(*refs):
        o_ref, g_ref, u_ref, d_ref, q_ref, k_ref, v_ref, ga_ref, gf_ref = refs[8:]
        x = sum(ref[...].astype(F32) for ref in refs[4:8])
        q_ref[...] = x[:ROWS_D, :72]
        k_ref[...] = x[:ROWS_D, 72:96].T
        v_ref[...] = x[:ROWS_D, 96:120].T
        ga_ref[...] = x[ROWS_D : ROWS_D + 1, :72]
        gf_ref[...] = x[ROWS_D + 1 : ROWS_D + 2, :72]
        x = sum(ref[...].astype(F32) for ref in refs[:4])
        wide = x[:ROWS_D]
        g_ref[...] = jnp.concatenate([wide[:, :128], wide[:, 256:320]], axis=1)
        u_ref[...] = jnp.concatenate([wide[:, 128:256], wide[:, 320:]], axis=1)
        for g, (start, count) in enumerate(FOLDS):
            o_ref[start : start + count, :] = x[144 : 144 + count, 72 * g : 72 * g + 72]
        low = x[176:248]
        d_ref[...] = jnp.concatenate(
            [low[:, :128], low[:, 256:320], low[:, 128:256], low[:, 320:]], axis=1
        )

    shapes = [(ROWS_D, 72), (ROWS_D, 192), (ROWS_D, 192), (72, 384)]
    shapes += [(ROWS_D, 72), (24, ROWS_D), (24, ROWS_D), (1, 72), (1, 72)]
    terms = [*terms_f, *terms_a]
    return call(
        body,
        (1,),
        [whole(x.shape) for x in terms],
        [whole(s) for s in shapes],
        [sds(s, F32) for s in shapes],
    )(*terms)


def pick_slots(coords, x):
    slots, width, rows = x.shape

    def body(co, x_ref, *outs):
        for d in range(slots):
            outs[d][...] = x_ref[lax.rem(co[1] + d, slots)]

    return call(
        body,
        (1,),
        [SMEM_SPEC, whole(x.shape)],
        [whole((width, rows))] * slots,
        [sds((width, rows), BF)] * slots,
    )(coords, x)


def place_slots(coords, pieces, dtype):
    slots = len(pieces)
    width, rows = pieces[0].shape

    def body(co, *refs):
        for d in range(slots):
            refs[slots][lax.rem(co[1] - d + slots, slots)] = refs[d][...].astype(dtype)

    return call(
        body,
        (1,),
        [SMEM_SPEC] + [whole((width, rows))] * slots,
        [whole((slots, width, rows))],
        [sds((slots, width, rows), dtype)],
    )(coords, *pieces)[0]


def redeal(pieces, ctx, group):
    return [pieces[0]] + [
        lax.ppermute(pieces[d], "ctx", shifted(ctx, group, d))
        for d in range(1, len(pieces))
    ]


def exchange(kv, ctx, group):
    return [kv] + [lax.ppermute(kv, "ctx", within(ctx, group, e)) for e in range(1, group)]


def after(x, mark):
    return lax.optimization_barrier((x, mark))[0]


def tables(slots, block, group):
    c = lax.axis_index("ctx") % group
    half_width = HD // 2
    frequency = jnp.exp(jnp.arange(half_width, dtype=F32) * (-2.0 * math.log(10000.0) / HD))
    positions = (group * jnp.arange(slots)[:, None] + c) * block + jnp.arange(block)[None, :]
    angles = positions.reshape(-1).astype(F32)[:, None] * frequency[None, :]
    cosine, sine = jnp.cos(angles), jnp.sin(angles)
    return (
        jnp.concatenate([cosine] * 4, axis=1),
        jnp.concatenate([-sine, sine, -sine, sine], axis=1),
    )


def gather_matrix(shard):
    return lax.all_gather(
        lax.all_gather(shard, "ctx", axis=1, tiled=True), "dp", axis=0, tiled=True
    )


def scatter_matrix(grad):
    part = lax.psum_scatter(grad, "dp", scatter_dimension=0, tiled=True)
    return lax.psum_scatter(part, "ctx", scatter_dimension=1, tiled=True).astype(F32)


def step(
    tokens,
    prefix,
    norm_attn,
    w_query,
    w_key,
    w_value,
    w_output,
    norm_ffn,
    w_gate,
    w_up,
    w_down,
    cotangent,
):
    slots, _, block, width = tokens.shape
    ctx = lax.axis_size("ctx")
    group = ctx // slots
    index = lax.axis_index("ctx")
    c = index % group
    cs, sn = tables(slots, block, group)
    micro_prefix = lax.dynamic_index_in_dim(prefix[:, 0], index // group, 0, keepdims=True)
    members = (c - jnp.arange(group)) % group
    meta = jnp.concatenate([micro_prefix, members]).astype(jnp.int32)

    dp = lax.axis_size("dp")
    coords = jnp.stack([lax.axis_index("dp"), index // group, c]).astype(jnp.int32)
    tight = dp == 4 and ctx == 8 and slots == 4 and w_query.shape == (ROWS_D, 72)

    own_tokens = jnp.swapaxes(tokens[:, 0], 1, 2)
    if tight:
        shards = (w_query, w_key.T, w_value.T, w_output, w_gate, w_up, w_down.T)
        pack_a, pack_top, pack_low = pack_shards(shards + (norm_attn[None], norm_ffn[None]))
        stack_a = spread_z(pack_a)
        picked = pick_slots(coords, after(own_tokens, pack_a))
        h = redeal(picked, ctx, group)
        w_qkv, gains = assemble_attn(coords, spread_attn(stack_a, (cs, sn, meta)))
        spread = spread_ffn(spread_z(pack_top), spread_z(pack_low))
        w_out, *w_ffn = assemble_ffn(coords, spread)
    else:
        gains = lax.all_gather(jnp.stack([norm_attn, norm_ffn]), "ctx", axis=1, tiled=True)
        gains = jnp.concatenate([gains.astype(F32), jnp.zeros((14, width), F32)], axis=0)
        w_qkv = jnp.concatenate(
            [gather_matrix(w_query), gather_matrix(w_key), gather_matrix(w_value)], axis=1
        )
        h = redeal(pick_slots(coords, own_tokens), ctx, group)
        w_out = gather_matrix(w_output)
        w_ffn = [gather_matrix(w_gate), gather_matrix(w_up), gather_matrix(w_down).T]
    full = (w_out, gains, *w_ffn)

    kept = []
    for layer in range(2):
        last = layer == 1
        na, q, kv, *dealt = qkv_forward(h, gains, w_qkv, cs, sn, None if last else coords)
        if dealt:
            h = dealt[0]
        kv_parts = exchange(kv, ctx, group)
        att, linv, *probs = attend_forward(q, kv_parts, meta, slots)
        h1, nb, a, b, hid, h2, *out_pieces = ffn_forward(
            h, att, *full, coords if last else None, slots
        )
        kept.append((h, na, q, kv_parts, att, linv, probs, h1, nb, a, b, hid))
        h = h2

    g = pick_slots(coords, jnp.swapaxes(cotangent[:, 0], 1, 2))
    g = redeal(g, ctx, group)
    out_pieces = redeal(out_pieces, ctx, group)
    block_output = place_slots(coords, out_pieces, BF)
    before_ffn = None
    for layer in (1, 0):
        h, na, q, kv_parts, att, linv, probs, h1, nb, a, b, hid = kept[layer]
        *before_ffn, g1, datt = ffn_backward(
            g, (h1, nb, a, b, hid, att), full, before_ffn, coords if layer == 1 else None
        )
        back_args = (q, kv_parts, datt, att, linv, probs, cs, sn, slots)
        chunks = [(0, KV)] if layer == 1 else [(0, 1), (1, KV - 1)]
        if layer == 0 and tight:
            grad_down, grad_gate, grad_up, grad_out, gn_ffn = before_ffn
            parts_f = split_ffn(coords, grad_out, grad_gate, grad_up, grad_down)
            terms_f, marks = sum_ffn(parts_f)
        dq, sent = [], []
        for n, (first, count) in enumerate(chunks):
            args = back_args
            if layer == 0 and tight:
                args = (after(q, marks[n]),) + back_args[1:]
            got = attend_backward(*args, first, count)
            dq.append(got[0])
            sent.append(got[1:])
        own = [parts[0] for parts in sent]
        moved = [
            lax.ppermute(parts[e], "ctx", within(ctx, group, -e))
            for e in range(1, group)
            for parts in sent
        ]
        dkv = own + moved
        back = (dq, dkv, na, h, g1, gains, w_qkv, cs, sn)
        if layer == 1:
            before_qkv, gn_attn, g = qkv_backward(*back, None)
        else:
            d_qkv, gn_attn, *g = qkv_backward(*back, gn_attn, coords, slots)
    input_grad = place_slots(coords, redeal(g, ctx, group), F32)
    grad_down, grad_gate, grad_up, grad_out, gn_ffn = before_ffn
    if tight:
        split = split_attn(coords, d_qkv, na, before_qkv, gn_attn, gn_ffn)
        done = finish(terms_f, sum_attn(split))
        g_out, g_gate, g_up, g_down, g_query, g_key, g_value, gn_attn, gn_ffn = done
        g_key, g_value, g_down = g_key.T, g_value.T, g_down.T
        gn = (gn_attn[0], gn_ffn[0])
    else:
        gn = lax.psum(jnp.concatenate([gn_attn, gn_ffn], axis=0), "dp")
        gn = lax.psum_scatter(gn, "ctx", scatter_dimension=1, tiled=True)
        grad_qkv = qkv_weights(d_qkv, na, before_qkv)
        g_query = scatter_matrix(grad_qkv[:, :WQ])
        g_key = scatter_matrix(grad_qkv[:, WQ : WQ + WK])
        g_value = scatter_matrix(grad_qkv[:, WQ + WK :])
        g_out = scatter_matrix(grad_out)
        g_gate, g_up, g_down = [scatter_matrix(x) for x in (grad_gate, grad_up, grad_down.T)]
    return (
        jnp.swapaxes(block_output, 1, 2)[:, None],
        jnp.swapaxes(input_grad, 1, 2)[:, None],
        gn[0],
        g_query,
        g_key,
        g_value,
        g_out,
        gn[1],
        g_gate,
        g_up,
        g_down,
    )


def solution(mesh):
    act = P(None, "dp", "ctx", None)
    mat = P("dp", "ctx")
    in_specs = (act, P(None, "dp"), P("ctx"), mat, mat, mat, mat, P("ctx"), mat, mat, mat, act)
    out_specs = (act, act, P("ctx"), mat, mat, mat, mat, P("ctx"), mat, mat, mat)
    return jax.shard_map(step, mesh=mesh, in_specs=in_specs, out_specs=out_specs, check_vma=False)
```

profile of v0, /device:TPU:0, one launch (start us, length us, event | category | flops | bytes accessed | tf_op | source)
XLA Modules:
  0.0 315.2 jit_solution(12611543749447903730)
XLA Ops:
  0.7 1.9 shard_map.203
  2.5 5.1 %collective-permute-start.5 = (bf16[160,128]{1,0:T(8,128)(2,1)}, bf16[160,128]{1,0:T(8,128)(2,1)S(1)}, u32[]{:S(2)}, u32[]{:S(2)}) collective-permute-start(bf16[160,128]{1,0:T(8,128)(2,1)} %get-tuple-element.119), channel_id=1, source_target_pairs={{0,6},{1,7},{2,0},{3,1},{4,2},{5,3},{6,4},{7,5},{8,14},{9,15},{10,... | collective-permute-start | bytes 122888 | tf_op jit(solution)/shard_map/ppermute | solution.py:633
  8.7 2.8 collective-permute-start.22
  17.0 3.2 %collective-permute-start.14 = (bf16[144,384]{1,0:T(8,128)(2,1)S(1)}, bf16[144,384]{1,0:T(8,128)(2,1)S(1)}, u32[]{:S(2)}, u32[]{:S(2)}) collective-permute-start(bf16[144,384]{1,0:T(8,128)(2,1)S(1)} %copy-done.54), channel_id=1, source_target_pairs={{0,2},{1,3},{2,4},{3,5},{4,6},{5,7},{6,0},{7,1},{8,10},{9,11},{10,... | collective-permute-start | bytes 331784 | tf_op jit(solution)/shard_map/ppermute | solution.py:633
  20.2 2.5 collective-permute-start.8
  25.1 1.9 shard_map.204
  28.2 3.4 %collective-permute-start = (bf16[576,128]{1,0:T(8,128)(2,1)}, bf16[576,128]{1,0:T(8,128)(2,1)S(1)}, u32[]{:S(2)}, u32[]{:S(2)}) collective-permute-start(bf16[576,128]{1,0:T(8,128)(2,1)} %get-tuple-element.122), channel_id=1, source_target_pairs={{0,2},{1,3},{2,4},{3,5},{4,6},{5,7},{6,0},{7,1},{8,10},{9,11},{10,... | collective-permute-start | bytes 442376 | tf_op jit(solution)/shard_map/ppermute | solution.py:930
  34.6 3.7 %collective-permute-start.2 = (bf16[576,128]{1,0:T(8,128)(2,1)}, bf16[576,128]{1,0:T(8,128)(2,1)S(1)}, u32[]{:S(2)}, u32[]{:S(2)}) collective-permute-start(bf16[576,128]{1,0:T(8,128)(2,1)} %get-tuple-element.124), channel_id=1, source_target_pairs={{0,6},{1,7},{2,0},{3,1},{4,2},{5,3},{6,4},{7,5},{8,14},{9,15},{10,... | collective-permute-start | bytes 442376 | tf_op jit(solution)/shard_map/ppermute | solution.py:930
  38.4 3.7 %collective-permute-done.20 = bf16[112,384]{1,0:T(8,128)(2,1)S(1)} collective-permute-done((bf16[112,384]{1,0:T(8,128)(2,1)S(1)}, bf16[112,384]{1,0:T(8,128)(2,1)S(1)}, u32[]{:S(2)}, u32[]{:S(2)}) %collective-permute-start.20) | collective-permute-done | bytes 86048 | tf_op jit(solution)/shard_map/ppermute | solution.py:633
  49.2 3.3 %collective-permute-done.17.refs_1_ = bf16[4,144,384]{2,1,0:T(8,128)(2,1)S(1)} collective-permute-done((bf16[4,144,384]{2,1,0:T(8,128)(2,1)S(1)}, bf16[4,144,384]{2,1,0:T(8,128)(2,1)S(1)}, u32[]{:S(2)}, u32[]{:S(2)}) %collective-permute-start.17) | collective-permute-done | bytes 442400 | tf_op jit(solution)/shard_map/ppermute | solution.py:645
  52.5 2.1 collective-permute-start.19
  54.7 3.4 %shard_map.205 = (bf16[576,960]{1,0:T(8,128)(2,1)}, f32[16,576]{1,0:T(8,128)}) custom-call(s32[3]{0:T(128)} %pad_add_fusion.co.refs_0_, bf16[4,160,128]{2,1,0:T(8,128)(2,1)} %copy-done.10, bf16[4,160,128]{2,1,0:T(8,128)(2,1)} %copy-done.32, bf16[4,160,128]{2,1,0:T(8,128)(2,1)} %copy-done.31, bf16[4,160,128]{2,1,0:T(8,128)(2,1)} %copy-done.30, ...), custom_call_target="tpu_custom_call" | custom-call | tf_op jit(solution)/shard_map/pallas_call | solution.py:681
  58.0 4.7 %shard_map.206 = (bf16[512,576]{1,0:T(8,128)(2,1)}, bf16[9,512,128]{2,1,0:T(8,128)(2,1)}, bf16[3,512,128]{2,1,0:T(8,128)(2,1)}, f32[512,576]{1,0:T(8,128)}) custom-call(s32[3]{0:T(128)} %pad_add_fusion.co.refs_0_, bf16[576,128]{1,0:T(8,128)(2,1)} %get-tuple-element.121.refs_1_, bf16[576,128]{1,0:T(8,128)(2,1)} %copy-done.41, bf16[576,128]{1,0:T(8,128)(2,1)} %copy-done.42, ...), custom_call_target="tpu_custom_call" | custom-call | tf_op jit(solution)/shard_map/pallas_call | solution.py:115
  66.1 8.0 %collective-permute-done.19.refs_3_ = bf16[4,144,384]{2,1,0:T(8,128)(2,1)S(1)} collective-permute-done((bf16[4,144,384]{2,1,0:T(8,128)(2,1)S(1)}, bf16[4,144,384]{2,1,0:T(8,128)(2,1)S(1)}, u32[]{:S(2)}, u32[]{:S(2)}) %collective-permute-start.19) | collective-permute-done | bytes 442400 | tf_op jit(solution)/shard_map/ppermute | solution.py:649
  74.7 10.6 %shard_map.207 = (bf16[3,512,192]{2,1,0:T(8,128)(2,1)}, f32[3,512,128]{2,1,0:T(8,128)}, bf16[3,512,384]{2,1,0:T(8,128)(2,1)}, bf16[3,512,384]{2,1,0:T(8,128)(2,1...) custom-call(s32[3]{0:T(128)} %pad_add_fusion.1.meta_ref, bf16[9,512,128]{2,1,0:T(8,128)(2,1)} %get-tuple-element.195.q_ref, ...), custom_call_target="tpu_custom_call" | custom-call | tf_op jit(solution)/shard_map/pallas_call | solution.py:200
  87.3 6.3 %shard_map.208 = (bf16[576,576]{1,0:T(8,128)(2,1)}, bf16[576,1536]{1,0:T(8,128)(2,1)}, bf16[576,1536]{1,0:T(8,128)(2,1)}, bf16[576,1536]{1,0:T(8,128)(2,1)}) custom-call(s32[3]{0:T(128)} %pad_add_fusion.co.refs_0_, bf16[4,144,384]{2,1,0:T(8,128)(2,1)} %copy-done.3, bf16[4,144,384]{2,1,0:T(8,128)(2,1)} %copy-done.11, bf16[4,144,384]{2,1,0:T(8,128)(2,1)} %copy-done.13, ...), custom_call_target="tpu_custom_call" | custom-call | tf_op jit(solution)/shard_map/pallas_call | solution.py:729
  93.6 9.8 %shard_map.209 = (f32[512,576]{1,0:T(8,128)}, bf16[512,576]{1,0:T(8,128)(2,1)}, bf16[512,1536]{1,0:T(8,128)(2,1)}, bf16[512,1536]{1,0:T(8,128)(2,1)}, bf16[512,1536]{1,0:T(8,128)(2,1)}, /*index=5*/f32[512,576]{1,0:T(8,128)}) custom-call(f32[512,576]{1,0:T(8,128)} %get-tuple-element.130.refs_0_.refs_8_, ...), custom_call_target="tpu_custom_call" | custom-call | tf_op jit(solution)/shard_map/pallas_call | solution.py:360
  103.4 4.5 %shard_map.210 = (bf16[512,576]{1,0:T(8,128)(2,1)}, bf16[9,512,128]{2,1,0:T(8,128)(2,1)}, bf16[3,512,128]{2,1,0:T(8,128)(2,1)}) custom-call(f32[512,576]{1,0:T(8,128)} %get-tuple-element.140.refs_0_.refs_1_.refs_4_, f32[16,576]{1,0:T(8,128)} %get-tuple-element.128.refs_5_.refs_3_.refs_1_.refs_4_.refs_11_.refs_6_.refs_7_.refs_10_, ...), custom_call_target="tpu_custom_call" | custom-call | tf_op jit(solution)/shard_map/pallas_call | solution.py:115
  108.4 1.9 shard_map.214
  110.3 4.0 %collective-permute-start.38 = (bf16[576,128]{1,0:T(8,128)(2,1)}, bf16[576,128]{1,0:T(8,128)(2,1)S(1)}, u32[]{:S(2)}, u32[]{:S(2)}) collective-permute-start(bf16[576,128]{1,0:T(8,128)(2,1)} %get-tuple-element.149), channel_id=1, source_target_pairs={{0,2},{1,3},{2,4},{3,5},{4,6},{5,7},{6,0},{7,1},{8,10},{9,11},{10,... | collective-permute-start | bytes 442376 | tf_op jit(solution)/shard_map/ppermute | solution.py:930
  114.3 1.9 collective-permute-start.39
  116.2 2.9 collective-permute-start.40
  119.9 10.6 %shard_map.211 = (bf16[3,512,192]{2,1,0:T(8,128)(2,1)}, f32[3,512,128]{2,1,0:T(8,128)}, bf16[3,512,384]{2,1,0:T(8,128)(2,1)}, bf16[3,512,384]{2,1,0:T(8,128)(2,1...) custom-call(s32[3]{0:T(128)} %pad_add_fusion.1.meta_ref, bf16[9,512,128]{2,1,0:T(8,128)(2,1)} %get-tuple-element.141.q_ref, ...), custom_call_target="tpu_custom_call" | custom-call | tf_op jit(solution)/shard_map/pallas_call | solution.py:200
  130.6 11.2 %shard_map.212 = (f32[512,576]{1,0:T(8,128)}, bf16[512,576]{1,0:T(8,128)(2,1)}, bf16[512,1536]{1,0:T(8,128)(2,1)}, bf16[512,1536]{1,0:T(8,128)(2,1)}, bf16[512,1...) custom-call(s32[3]{0:T(128)} %pad_add_fusion.co.refs_0_, ...), custom_call_target="tpu_custom_call" | custom-call | tf_op jit(solution)/shard_map/pallas_call | solution.py:360
  142.5 17.1 %shard_map.215 = (f32[576,1536]{1,0:T(8,128)}, f32[576,1536]{1,0:T(8,128)}, f32[576,1536]{1,0:T(8,128)}, f32[576,576]{1,0:T(8,128)}, f32[1,576]{1,0:T(1,128)}, /...) custom-call(s32[3]{0:T(128)} %pad_add_fusion.co.refs_0_, bf16[576,128]{1,0:T(8,128)(2,1)} %get-tuple-element.148.refs_1_, ...), custom_call_target="tpu_custom_call" | custom-call | tf_op jit(solution)/shard_map/pallas_call | solution.py:459
  159.6 14.0 %shard_map.216 = (bf16[3,512,192]{2,1,0:T(8,128)(2,1)}, bf16[3,512,128]{2,1,0:T(8,128)(2,1)}, bf16[3,512,128]{2,1,0:T(8,128)(2,1)}) custom-call(bf16[9,512,128]{2,1,0:T(8,128)(2,1)} %get-tuple-element.141.q_ref, bf16[3,512,192]{2,1,0:T(8,128)(2,1)} %get-tuple-element.157.datt_ref, bf16[3,512,192]{2,1,0:T(8,128)(2,1)} %get-tuple-element.143.refs_2_.refs_10_.att_ref, ...), custom_call_target="tpu_custom_call" | custom-call | tf_op jit(solution)/shard_map/pallas_call | solution.py:284
  173.7 1.9 collective-permute-done.41.refs_2_
  176.4 6.5 %shard_map.217 = (f32[576,960]{1,0:T(8,128)}, f32[1,576]{1,0:T(1,128)}, f32[512,576]{1,0:T(8,128)}) custom-call(bf16[3,512,192]{2,1,0:T(8,128)(2,1)} %get-tuple-element.163.refs_0_, bf16[3,512,128]{2,1,0:T(8,128)(2,1)} %get-tuple-element.164.refs_1_, bf16[3,512,128]{2,1,0:T(8,128)(2,1)} %copy-done.18, bf16[512,576]{1,0:T(8,128)(2,1)} %get-tuple-element.166.refs_3_, ...), custom_call_target="tpu_custom_call" | custom-call | tf_op jit(solution)/shard_map/pallas_call | solution.py:547
  182.9 19.2 %shard_map.218 = (bf16[576,1536]{1,0:T(8,128)(2,1)}, bf16[576,1536]{1,0:T(8,128)(2,1)}, bf16[576,1536]{1,0:T(8,128)(2,1)}, bf16[576,576]{1,0:T(8,128)(2,1)}, f32...) custom-call(f32[512,576]{1,0:T(8,128)} %get-tuple-element.168.refs_0_, ...), custom_call_target="tpu_custom_call" | custom-call | tf_op jit(solution)/shard_map/pallas_call | solution.py:459
  202.1 6.9 %shard_map.219 = (bf16[4,256,384]{2,1,0:T(8,128)(2,1)}, bf16[4,256,384]{2,1,0:T(8,128)(2,1)}, bf16[4,256,384]{2,1,0:T(8,128)(2,1)}, bf16[4,256,384]{2,1,0:T(8,128)(2,1)}, bf16[4,4,256,384]{3,2,1,0:T(8,128)(2,1)}) custom-call(s32[3]{0:T(128)} %pad_add_fusion.co.refs_0_, bf16[576,576]{1,0:T(8,128)(2,1)} %get-tuple-element.179.go, ...), custom_call_target="tpu_custom_call" | custom-call | tf_op jit(solution)/shard_map/pallas_call | solution.py:815
  209.1 5.7 %collective-permute-done.42 = bf16[4,4,256,384]{3,2,1,0:T(8,128)(2,1)S(1)} collective-permute-done((bf16[4,4,256,384]{3,2,1,0:T(8,128)(2,1)}, bf16[4,4,256,384]{3,2,1,0:T(8,128)(2,1)S(1)}, u32[]{:S(2)}, u32[]{:S(2)}) %collective-permute-start.42) | collective-permute-done | bytes 3145760 | tf_op jit(solution)/shard_map/ppermute | solution.py:844
  216.8 10.3 %shard_map.221 = (bf16[2,512,192]{2,1,0:T(8,128)(2,1)}, bf16[2,512,128]{2,1,0:T(8,128)(2,1)}, bf16[2,512,128]{2,1,0:T(8,128)(2,1)}) custom-call(bf16[9,512,128]{2,1,0:T(8,128)(2,1)} %get-tuple-element.195.q_ref, bf16[3,512,192]{2,1,0:T(8,128)(2,1)} %get-tuple-element.185.datt_ref, bf16[3,512,192]{2,1,0:T(8,128)(2,1)} %get-tuple-element.133.refs_1_.refs_6_.att_ref, ...), custom_call_target="tpu_custom_call" | custom-call | tf_op jit(solution)/shard_map/pallas_call | solution.py:284
  227.2 6.3 %shard_map.220 = (bf16[1,512,192]{2,1,0:T(8,128)(2,1)}, bf16[1,512,128]{2,1,0:T(8,128)(2,1)}, bf16[1,512,128]{2,1,0:T(8,128)(2,1)}) custom-call(bf16[9,512,128]{2,1,0:T(8,128)(2,1)} %get-tuple-element.195.q_ref, bf16[3,512,192]{2,1,0:T(8,128)(2,1)} %get-tuple-element.185.datt_ref, bf16[3,512,192]{2,1,0:T(8,128)(2,1)} %get-tuple-element.133.refs_1_.refs_6_.att_ref, ...), custom_call_target="tpu_custom_call" | custom-call | tf_op jit(solution)/shard_map/pallas_call | solution.py:284
  236.2 5.5 %shard_map.222 = (bf16[512,960]{1,0:T(8,128)(2,1)}, f32[1,576]{1,0:T(1,128)}, bf16[576,128]{1,0:T(8,128)(2,1)}, bf16[576,128]{1,0:T(8,128)(2,1)}, bf16[576,128]{1,0:T(8,128)(2,1)}, /*index=5*/bf16[576,128]{1,0:T(8,128)(2,1)}) custom-call(s32[3]{0:T(128)} %pad_add_fusion.co.refs_0_, bf16[1,512,192]{2,1,0:T(8,128)(2,1)} %get-tuple-element.191.refs_1_, ...), custom_call_target="tpu_custom_call" | custom-call | tf_op jit(solution)/shard_map/pallas_call | solution.py:547
  241.7 5.2 %shard_map.224 = (bf16[4,160,128]{2,1,0:T(8,128)(2,1)}, bf16[4,160,128]{2,1,0:T(8,128)(2,1)}, bf16[4,160,128]{2,1,0:T(8,128)(2,1)}, bf16[4,160,128]{2,1,0:T(8,128)(2,1)}, bf16[4,4,160,128]{3,2,1,0:T(8,128)(2,1)}) custom-call(s32[3]{0:T(128)} %pad_add_fusion.co.refs_0_, bf16[512,960]{1,0:T(8,128)(2,1)} %get-tuple-element.209.d_ref, ...), custom_call_target="tpu_custom_call" | custom-call | tf_op jit(solution)/shard_map/pallas_call | solution.py:771
  250.1 8.0 %collective-permute-done.53 = bf16[4,112,384]{2,1,0:T(8,128)(2,1)S(1)} collective-permute-done((bf16[4,112,384]{2,1,0:T(8,128)(2,1)S(1)}, bf16[4,112,384]{2,1,0:T(8,128)(2,1)S(1)}, u32[]{:S(2)}, u32[]{:S(2)}) %collective-permute-start.53) | collective-permute-done | bytes 344096 | tf_op jit(solution)/shard_map/ppermute | solution.py:858
  260.5 6.5 %collective-permute-done.50 = bf16[4,144,384]{2,1,0:T(8,128)(2,1)S(1)} collective-permute-done((bf16[4,144,384]{2,1,0:T(8,128)(2,1)S(1)}, bf16[4,144,384]{2,1,0:T(8,128)(2,1)S(1)}, u32[]{:S(2)}, u32[]{:S(2)}) %collective-permute-start.50) | collective-permute-done | bytes 442400 | tf_op jit(solution)/shard_map/ppermute | solution.py:855
  267.0 2.0 collective-permute-start.60
  269.0 2.1 collective-permute-done.49
  274.5 2.9 collective-permute-done.60
  278.8 2.6 collective-permute-start.47
  283.4 2.5 collective-permute-done.45.refs_1_
  286.6 2.7 collective-permute-done.46.refs_2_
  289.3 8.9 %collective-permute-start.63 = (bf16[160,128]{1,0:T(8,128)(2,1)S(1)}, bf16[160,128]{1,0:T(8,128)(2,1)S(1)}, u32[]{:S(2)}, u32[]{:S(2)}) collective-permute-start(bf16[160,128]{1,0:T(8,128)(2,1)S(1)} %get-tuple-element.260), channel_id=1, source_target_pairs={{0,6},{1,7},{2,0},{3,1},{4,2},{5,3},{6,4},{7,5},{8,14},{9,15},{10,... | collective-permute-start | bytes 122888 | tf_op jit(solution)/shard_map/ppermute | solution.py:832
  298.3 9.2 %collective-permute-start.61 = (bf16[160,128]{1,0:T(8,128)(2,1)S(1)}, bf16[160,128]{1,0:T(8,128)(2,1)S(1)}, u32[]{:S(2)}, u32[]{:S(2)}) collective-permute-start(bf16[160,128]{1,0:T(8,128)(2,1)S(1)} %get-tuple-element.262), channel_id=1, source_target_pairs={{0,2},{1,3},{2,4},{3,5},{4,6},{5,7},{6,0},{7,1},{8,10},{9,11},{10,... | collective-permute-start | bytes 122888 | tf_op jit(solution)/shard_map/ppermute | solution.py:832
  307.5 2.0 shard_map.213
  309.5 2.2 shard_map.223
  312.6 2.4 shard_map.225
  (260 shorter events, 47.3 us)
Async XLA Ops:
  2.5 12.5 %collective-permute-start.5 = (bf16[160,128]{1,0:T(8,128)(2,1)}, bf16[160,128]{1,0:T(8,128)(2,1)S(1)}, u32[]{:S(2)}, u32[]{:S(2)}) collective-permute-start(bf16[160,128]{1,0:T(8,128)(2,1)} %get-tuple-element.119), channel_id=1, source_target_pairs={{0,6},{1,7},{2,0},{3,1},{4,2},{5,3},{6,4},{7,5},{8,14},{9,15},{10,... | collective-permute-start | bytes 122888 | tf_op jit(solution)/shard_map/ppermute | solution.py:633
  7.7 9.3 %collective-permute-start.3 = (bf16[160,128]{1,0:T(8,128)(2,1)}, bf16[160,128]{1,0:T(8,128)(2,1)S(1)}, u32[]{:S(2)}, u32[]{:S(2)}) collective-permute-start(bf16[160,128]{1,0:T(8,128)(2,1)} %get-tuple-element.119), channel_id=1, source_target_pairs={{0,2},{1,3},{2,4},{3,5},{4,6},{5,7},{6,0},{7,1},{8,10},{9,11},{10,... | collective-permute-start | bytes 122888 | tf_op jit(solution)/shard_map/ppermute | solution.py:633
  8.7 11.5 %collective-permute-start.22 = (bf16[112,384]{1,0:T(8,128)(2,1)}, bf16[112,384]{1,0:T(8,128)(2,1)S(1)}, u32[]{:S(2)}, u32[]{:S(2)}) collective-permute-start(bf16[112,384]{1,0:T(8,128)(2,1)} %get-tuple-element.135), channel_id=1, source_target_pairs={{0,6},{1,7},{2,0},{3,1},{4,2},{5,3},{6,4},{7,5},{8,14},{9,15},{10,... | collective-permute-start | bytes 258056 | tf_op jit(solution)/shard_map/ppermute | solution.py:633
  11.5 11.2 %collective-permute-start.21 = (bf16[112,384]{1,0:T(8,128)(2,1)}, bf16[112,384]{1,0:T(8,128)(2,1)S(1)}, u32[]{:S(2)}, u32[]{:S(2)}) collective-permute-start(bf16[112,384]{1,0:T(8,128)(2,1)} %get-tuple-element.135), channel_id=1, source_target_pairs={{0,4},{1,5},{2,6},{3,7},{4,0},{5,1},{6,2},{7,3},{8,12},{9,13},{10,... | collective-permute-start | bytes 258056 | tf_op jit(solution)/shard_map/ppermute | solution.py:633
  16.0 12.3 %collective-permute-start.15 = (bf16[144,384]{1,0:T(8,128)(2,1)S(1)}, bf16[144,384]{1,0:T(8,128)(2,1)S(1)}, u32[]{:S(2)}, u32[]{:S(2)}) collective-permute-start(bf16[144,384]{1,0:T(8,128)(2,1)S(1)} %copy-done.54), channel_id=1, source_target_pairs={{0,4},{1,5},{2,6},{3,7},{4,0},{5,1},{6,2},{7,3},{8,12},{9,13},{10,... | collective-permute-start | bytes 331784 | tf_op jit(solution)/shard_map/ppermute | solution.py:633
  17.0 14.7 %collective-permute-start.14 = (bf16[144,384]{1,0:T(8,128)(2,1)S(1)}, bf16[144,384]{1,0:T(8,128)(2,1)S(1)}, u32[]{:S(2)}, u32[]{:S(2)}) collective-permute-start(bf16[144,384]{1,0:T(8,128)(2,1)S(1)} %copy-done.54), channel_id=1, source_target_pairs={{0,2},{1,3},{2,4},{3,5},{4,6},{5,7},{6,0},{7,1},{8,10},{9,11},{10,... | collective-permute-start | bytes 331784 | tf_op jit(solution)/shard_map/ppermute | solution.py:633
  20.2 14.2 %collective-permute-start.8 = (bf16[4,160,128]{2,1,0:T(8,128)(2,1)S(1)}, bf16[4,160,128]{2,1,0:T(8,128)(2,1)S(1)}, u32[]{:S(2)}, u32[]{:S(2)}) collective-permute-start(bf16[4,160,128]{2,1,0:T(8,128)(2,1)S(1)} %pad_maximum_fusion.5.refs_0_), channel_id=1, source_target_pairs={{0,24},{8,16},{16,8},{24,0},{1,25},{9,17},{17,9},{25,1},{2,26},{10... | collective-permute-start | bytes 491528 | tf_op jit(solution)/shard_map/ppermute | solution.py:638
  22.7 11.8 %collective-permute-start.7 = (bf16[4,160,128]{2,1,0:T(8,128)(2,1)S(1)}, bf16[4,160,128]{2,1,0:T(8,128)(2,1)S(1)}, u32[]{:S(2)}, u32[]{:S(2)}) collective-permute-start(bf16[4,160,128]{2,1,0:T(8,128)(2,1)S(1)} %pad_maximum_fusion.5.refs_0_), channel_id=1, source_target_pairs={{0,16},{8,24},{16,0},{24,8},{1,17},{9,25},{17,1},{25,9},{2,18},{10... | collective-permute-start | bytes 491528 | tf_op jit(solution)/shard_map/ppermute | solution.py:638
  23.2 15.1 %collective-permute-start.6 = (bf16[4,160,128]{2,1,0:T(8,128)(2,1)S(1)}, bf16[4,160,128]{2,1,0:T(8,128)(2,1)S(1)}, u32[]{:S(2)}, u32[]{:S(2)}) collective-permute-start(bf16[4,160,128]{2,1,0:T(8,128)(2,1)S(1)} %pad_maximum_fusion.5.refs_0_), channel_id=1, source_target_pairs={{0,8},{8,0},{16,24},{24,16},{1,9},{9,1},{17,25},{25,17},{2,10},{10... | collective-permute-start | bytes 491528 | tf_op jit(solution)/shard_map/ppermute | solution.py:638
  28.2 15.3 %collective-permute-start = (bf16[576,128]{1,0:T(8,128)(2,1)}, bf16[576,128]{1,0:T(8,128)(2,1)S(1)}, u32[]{:S(2)}, u32[]{:S(2)}) collective-permute-start(bf16[576,128]{1,0:T(8,128)(2,1)} %get-tuple-element.122), channel_id=1, source_target_pairs={{0,2},{1,3},{2,4},{3,5},{4,6},{5,7},{6,0},{7,1},{8,10},{9,11},{10,... | collective-permute-start | bytes 442376 | tf_op jit(solution)/shard_map/ppermute | solution.py:930
  31.6 12.1 %collective-permute-start.1 = (bf16[576,128]{1,0:T(8,128)(2,1)}, bf16[576,128]{1,0:T(8,128)(2,1)S(1)}, u32[]{:S(2)}, u32[]{:S(2)}) collective-permute-start(bf16[576,128]{1,0:T(8,128)(2,1)} %get-tuple-element.123), channel_id=1, source_target_pairs={{0,4},{1,5},{2,6},{3,7},{4,0},{5,1},{6,2},{7,3},{8,12},{9,13},{10,... | collective-permute-start | bytes 442376 | tf_op jit(solution)/shard_map/ppermute | solution.py:930
  34.6 10.0 %collective-permute-start.2 = (bf16[576,128]{1,0:T(8,128)(2,1)}, bf16[576,128]{1,0:T(8,128)(2,1)S(1)}, u32[]{:S(2)}, u32[]{:S(2)}) collective-permute-start(bf16[576,128]{1,0:T(8,128)(2,1)} %get-tuple-element.124), channel_id=1, source_target_pairs={{0,6},{1,7},{2,0},{3,1},{4,2},{5,3},{6,4},{7,5},{8,14},{9,15},{10,... | collective-permute-start | bytes 442376 | tf_op jit(solution)/shard_map/ppermute | solution.py:930
  42.1 10.4 %collective-permute-start.17 = (bf16[4,144,384]{2,1,0:T(8,128)(2,1)S(1)}, bf16[4,144,384]{2,1,0:T(8,128)(2,1)S(1)}, u32[]{:S(2)}, u32[]{:S(2)}) collective-permute-start(bf16[4,144,384]{2,1,0:T(8,128)(2,1)S(1)} %pad_maximum_fusion.refs_0_), channel_id=1, source_target_pairs={{0,8},{8,0},{16,24},{24,16},{1,9},{9,1},{17,25},{25,17},{2,10},{10... | collective-permute-start | bytes 1327112 | tf_op jit(solution)/shard_map/ppermute | solution.py:645
  45.1 17.6 %collective-permute-start.24 = (bf16[4,112,384]{2,1,0:T(8,128)(2,1)S(1)}, bf16[4,112,384]{2,1,0:T(8,128)(2,1)S(1)}, u32[]{:S(2)}, u32[]{:S(2)}) collective-permute-start(bf16[4,112,384]{2,1,0:T(8,128)(2,1)S(1)} %pad_maximum_fusion.1.refs_4_), channel_id=1, source_target_pairs={{0,16},{8,24},{16,0},{24,8},{1,17},{9,25},{17,1},{25,9},{2,18},{10... | collective-permute-start | bytes 1032200 | tf_op jit(solution)/shard_map/ppermute | solution.py:646
  46.5 16.8 %collective-permute-start.26 = (bf16[4,144,384]{2,1,0:T(8,128)(2,1)S(1)}, bf16[4,144,384]{2,1,0:T(8,128)(2,1)S(1)}, u32[]{:S(2)}, u32[]{:S(2)}) collective-permute-start(bf16[4,144,384]{2,1,0:T(8,128)(2,1)S(1)} %pad_maximum_fusion.refs_0_), channel_id=1, source_target_pairs={{0,1},{1,0},{2,3},{3,2},{4,5},{5,4},{6,7},{7,6},{8,9},{9,8},{10,11... | collective-permute-start | bytes 1327112 | tf_op jit(solution)/shard_map/ppermute | solution.py:652
  46.5 16.3 %collective-permute-start.23 = (bf16[4,112,384]{2,1,0:T(8,128)(2,1)S(1)}, bf16[4,112,384]{2,1,0:T(8,128)(2,1)S(1)}, u32[]{:S(2)}, u32[]{:S(2)}) collective-permute-start(bf16[4,112,384]{2,1,0:T(8,128)(2,1)S(1)} %pad_maximum_fusion.1.refs_4_), channel_id=1, source_target_pairs={{0,8},{8,0},{16,24},{24,16},{1,9},{9,1},{17,25},{25,17},{2,10},{10... | collective-permute-start | bytes 1032200 | tf_op jit(solution)/shard_map/ppermute | solution.py:648
  47.9 17.6 %collective-permute-start.18 = (bf16[4,144,384]{2,1,0:T(8,128)(2,1)S(1)}, bf16[4,144,384]{2,1,0:T(8,128)(2,1)S(1)}, u32[]{:S(2)}, u32[]{:S(2)}) collective-permute-start(bf16[4,144,384]{2,1,0:T(8,128)(2,1)S(1)} %pad_maximum_fusion.refs_0_), channel_id=1, source_target_pairs={{0,16},{8,24},{16,0},{24,8},{1,17},{9,25},{17,1},{25,9},{2,18},{10... | collective-permute-start | bytes 1327112 | tf_op jit(solution)/shard_map/ppermute | solution.py:647
  52.5 21.6 %collective-permute-start.19 = (bf16[4,144,384]{2,1,0:T(8,128)(2,1)S(1)}, bf16[4,144,384]{2,1,0:T(8,128)(2,1)S(1)}, u32[]{:S(2)}, u32[]{:S(2)}) collective-permute-start(bf16[4,144,384]{2,1,0:T(8,128)(2,1)S(1)} %collective-permute-done.17.refs_1_), channel_id=1, source_target_pairs={{0,16},{8,24},{16,0},{24,8},{1,17},{9,25},{17,1},{25,9},{2,18},{10... | collective-permute-start | bytes 1327112 | tf_op jit(solution)/shard_map/ppermute | solution.py:649
  62.8 11.3 %collective-permute-start.32 = (bf16[4,112,384]{2,1,0:T(8,128)(2,1)S(1)}, bf16[4,112,384]{2,1,0:T(8,128)(2,1)S(1)}, u32[]{:S(2)}, u32[]{:S(2)}) collective-permute-start(bf16[4,112,384]{2,1,0:T(8,128)(2,1)S(1)} %collective-permute-done.24.refs_6_), channel_id=1, source_target_pairs={{0,1},{1,0},{2,3},{3,2},{4,5},{5,4},{6,7},{7,6},{8,9},{9,8},{10,11... | collective-permute-start | bytes 1032200 | tf_op jit(solution)/shard_map/ppermute | solution.py:652
  63.3 11.3 %collective-permute-start.25 = (bf16[4,112,384]{2,1,0:T(8,128)(2,1)S(1)}, bf16[4,112,384]{2,1,0:T(8,128)(2,1)S(1)}, u32[]{:S(2)}, u32[]{:S(2)}) collective-permute-start(bf16[4,112,384]{2,1,0:T(8,128)(2,1)S(1)} %collective-permute-done.24.refs_6_), channel_id=1, source_target_pairs={{0,8},{8,0},{16,24},{24,16},{1,9},{9,1},{17,25},{25,17},{2,10},{10... | collective-permute-start | bytes 1032200 | tf_op jit(solution)/shard_map/ppermute | solution.py:650
  65.5 19.8 %collective-permute-start.28 = (bf16[4,144,384]{2,1,0:T(8,128)(2,1)S(1)}, bf16[4,144,384]{2,1,0:T(8,128)(2,1)S(1)}, u32[]{:S(2)}, u32[]{:S(2)}) collective-permute-start(bf16[4,144,384]{2,1,0:T(8,128)(2,1)S(1)} %collective-permute-done.18.refs_2_), channel_id=1, source_target_pairs={{0,1},{1,0},{2,3},{3,2},{4,5},{5,4},{6,7},{7,6},{8,9},{9,8},{10,11... | collective-permute-start | bytes 1327112 | tf_op jit(solution)/shard_map/ppermute | solution.py:652
  65.5 19.8 %collective-permute-start.27 = (bf16[4,144,384]{2,1,0:T(8,128)(2,1)S(1)}, bf16[4,144,384]{2,1,0:T(8,128)(2,1)S(1)}, u32[]{:S(2)}, u32[]{:S(2)}) collective-permute-start(bf16[4,144,384]{2,1,0:T(8,128)(2,1)S(1)} %collective-permute-done.17.refs_1_), channel_id=1, source_target_pairs={{0,1},{1,0},{2,3},{3,2},{4,5},{5,4},{6,7},{7,6},{8,9},{9,8},{10,11... | collective-permute-start | bytes 1327112 | tf_op jit(solution)/shard_map/ppermute | solution.py:652
  74.1 11.3 %collective-permute-start.29 = (bf16[4,144,384]{2,1,0:T(8,128)(2,1)S(1)}, bf16[4,144,384]{2,1,0:T(8,128)(2,1)S(1)}, u32[]{:S(2)}, u32[]{:S(2)}) collective-permute-start(bf16[4,144,384]{2,1,0:T(8,128)(2,1)S(1)} %collective-permute-done.19.refs_3_), channel_id=1, source_target_pairs={{0,1},{1,0},{2,3},{3,2},{4,5},{5,4},{6,7},{7,6},{8,9},{9,8},{10,11... | collective-permute-start | bytes 1327112 | tf_op jit(solution)/shard_map/ppermute | solution.py:652
  74.1 11.2 %collective-permute-start.31 = (bf16[4,112,384]{2,1,0:T(8,128)(2,1)S(1)}, bf16[4,112,384]{2,1,0:T(8,128)(2,1)S(1)}, u32[]{:S(2)}, u32[]{:S(2)}) collective-permute-start(bf16[4,112,384]{2,1,0:T(8,128)(2,1)S(1)} %collective-permute-done.23.refs_5_), channel_id=1, source_target_pairs={{0,1},{1,0},{2,3},{3,2},{4,5},{5,4},{6,7},{7,6},{8,9},{9,8},{10,11... | collective-permute-start | bytes 1032200 | tf_op jit(solution)/shard_map/ppermute | solution.py:652
  74.6 10.8 %collective-permute-start.33 = (bf16[4,112,384]{2,1,0:T(8,128)(2,1)S(1)}, bf16[4,112,384]{2,1,0:T(8,128)(2,1)S(1)}, u32[]{:S(2)}, u32[]{:S(2)}) collective-permute-start(bf16[4,112,384]{2,1,0:T(8,128)(2,1)S(1)} %collective-permute-done.25.refs_7_), channel_id=1, source_target_pairs={{0,1},{1,0},{2,3},{3,2},{4,5},{5,4},{6,7},{7,6},{8,9},{9,8},{10,11... | collective-permute-start | bytes 1032200 | tf_op jit(solution)/shard_map/ppermute | solution.py:652
  107.9 11.2 %collective-permute-start.34 = (bf16[3,512,128]{2,1,0:T(8,128)(2,1)}, bf16[3,512,128]{2,1,0:T(8,128)(2,1)S(1)}, u32[]{:S(2)}, u32[]{:S(2)}) collective-permute-start(bf16[3,512,128]{2,1,0:T(8,128)(2,1)} %get-tuple-element.142.refs_0_), channel_id=1, source_target_pairs={{0,1},{1,0},{2,3},{3,2},{4,5},{5,4},{6,7},{7,6},{8,9},{9,8},{10,11... | collective-permute-start | bytes 1179656 | tf_op jit(solution)/shard_map/ppermute | solution.py:936
  110.3 31.5 %collective-permute-start.38 = (bf16[576,128]{1,0:T(8,128)(2,1)}, bf16[576,128]{1,0:T(8,128)(2,1)S(1)}, u32[]{:S(2)}, u32[]{:S(2)}) collective-permute-start(bf16[576,128]{1,0:T(8,128)(2,1)} %get-tuple-element.149), channel_id=1, source_target_pairs={{0,2},{1,3},{2,4},{3,5},{4,6},{5,7},{6,0},{7,1},{8,10},{9,11},{10,... | collective-permute-start | bytes 442376 | tf_op jit(solution)/shard_map/ppermute | solution.py:930
  114.3 27.5 %collective-permute-start.39 = (bf16[576,128]{1,0:T(8,128)(2,1)}, bf16[576,128]{1,0:T(8,128)(2,1)S(1)}, u32[]{:S(2)}, u32[]{:S(2)}) collective-permute-start(bf16[576,128]{1,0:T(8,128)(2,1)} %get-tuple-element.150), channel_id=1, source_target_pairs={{0,4},{1,5},{2,6},{3,7},{4,0},{5,1},{6,2},{7,3},{8,12},{9,13},{10,... | collective-permute-start | bytes 442376 | tf_op jit(solution)/shard_map/ppermute | solution.py:930
  116.2 25.6 %collective-permute-start.40 = (bf16[576,128]{1,0:T(8,128)(2,1)}, bf16[576,128]{1,0:T(8,128)(2,1)S(1)}, u32[]{:S(2)}, u32[]{:S(2)}) collective-permute-start(bf16[576,128]{1,0:T(8,128)(2,1)} %get-tuple-element.151), channel_id=1, source_target_pairs={{0,6},{1,7},{2,0},{3,1},{4,2},{5,3},{6,4},{7,5},{8,14},{9,15},{10,... | collective-permute-start | bytes 442376 | tf_op jit(solution)/shard_map/ppermute | solution.py:930
  215.5 31.5 %collective-permute-start.52 = (bf16[4,112,384]{2,1,0:T(8,128)(2,1)S(1)}, bf16[4,112,384]{2,1,0:T(8,128)(2,1)S(1)}, u32[]{:S(2)}, u32[]{:S(2)}) collective-permute-start(bf16[4,112,384]{2,1,0:T(8,128)(2,1)S(1)} %add_convert_fusion.7), channel_id=1, source_target_pairs={{0,8},{8,0},{16,24},{24,16},{1,9},{9,1},{17,25},{25,17},{2,10},{10... | collective-permute-start | bytes 1032200 | tf_op jit(solution)/shard_map/ppermute | solution.py:853
  233.9 14.7 %collective-permute-start.48 = (bf16[4,144,384]{2,1,0:T(8,128)(2,1)S(1)}, bf16[4,144,384]{2,1,0:T(8,128)(2,1)S(1)}, u32[]{:S(2)}, u32[]{:S(2)}) collective-permute-start(bf16[4,144,384]{2,1,0:T(8,128)(2,1)S(1)} %add_convert_fusion.3), channel_id=1, source_target_pairs={{0,16},{8,24},{16,0},{24,8},{1,17},{9,25},{17,1},{25,9},{2,18},{10... | collective-permute-start | bytes 1327112 | tf_op jit(solution)/shard_map/ppermute | solution.py:852
  234.4 15.0 %collective-permute-start.51 = (bf16[4,112,384]{2,1,0:T(8,128)(2,1)S(1)}, bf16[4,112,384]{2,1,0:T(8,128)(2,1)S(1)}, u32[]{:S(2)}, u32[]{:S(2)}) collective-permute-start(bf16[4,112,384]{2,1,0:T(8,128)(2,1)S(1)} %add_convert_fusion.6), channel_id=1, source_target_pairs={{0,8},{8,0},{16,24},{24,16},{1,9},{9,1},{17,25},{25,17},{2,10},{10... | collective-permute-start | bytes 1032200 | tf_op jit(solution)/shard_map/ppermute | solution.py:854
  246.9 12.4 %collective-permute-start.57 = (bf16[4,4,160,128]{3,2,1,0:T(8,128)(2,1)}, bf16[4,4,160,128]{3,2,1,0:T(8,128)(2,1)S(1)}, u32[]{:S(2)}, u32[]{:S(2)}) collective-permute-start(bf16[4,4,160,128]{3,2,1,0:T(8,128)(2,1)} %get-tuple-element.214), channel_id=1, source_target_pairs={{0,1},{1,0},{2,3},{3,2},{4,5},{5,4},{6,7},{7,6},{8,9},{9,8},{10,11... | collective-permute-start | bytes 1966088 | tf_op jit(solution)/shard_map/ppermute | solution.py:837
  247.1 11.0 %collective-permute-start.53 = (bf16[4,112,384]{2,1,0:T(8,128)(2,1)S(1)}, bf16[4,112,384]{2,1,0:T(8,128)(2,1)S(1)}, u32[]{:S(2)}, u32[]{:S(2)}) collective-permute-start(bf16[4,112,384]{2,1,0:T(8,128)(2,1)S(1)} %add_convert_fusion.5), channel_id=1, source_target_pairs={{0,16},{8,24},{16,0},{24,8},{1,17},{9,25},{17,1},{25,9},{2,18},{10... | collective-permute-start | bytes 1032200 | tf_op jit(solution)/shard_map/ppermute | solution.py:858
  248.6 30.1 %collective-permute-start.35 = (bf16[576,128]{1,0:T(8,128)(2,1)S(1)}, bf16[576,128]{1,0:T(8,128)(2,1)S(1)}, u32[]{:S(2)}, u32[]{:S(2)}) collective-permute-start(bf16[576,128]{1,0:T(8,128)(2,1)S(1)} %copy-done.62), channel_id=1, source_target_pairs={{0,2},{1,3},{2,4},{3,5},{4,6},{5,7},{6,0},{7,1},{8,10},{9,11},{10,... | collective-permute-start | bytes 442376 | tf_op jit(solution)/shard_map/ppermute | solution.py:930
  248.7 32.7 %collective-permute-start.36 = (bf16[576,128]{1,0:T(8,128)(2,1)S(1)}, bf16[576,128]{1,0:T(8,128)(2,1)S(1)}, u32[]{:S(2)}, u32[]{:S(2)}) collective-permute-start(bf16[576,128]{1,0:T(8,128)(2,1)S(1)} %copy-done.61), channel_id=1, source_target_pairs={{0,4},{1,5},{2,6},{3,7},{4,0},{5,1},{6,2},{7,3},{8,12},{9,13},{10,... | collective-permute-start | bytes 442376 | tf_op jit(solution)/shard_map/ppermute | solution.py:930
  249.5 17.5 %collective-permute-start.50 = (bf16[4,144,384]{2,1,0:T(8,128)(2,1)S(1)}, bf16[4,144,384]{2,1,0:T(8,128)(2,1)S(1)}, u32[]{:S(2)}, u32[]{:S(2)}) collective-permute-start(bf16[4,144,384]{2,1,0:T(8,128)(2,1)S(1)} %add_convert_fusion.2), channel_id=1, source_target_pairs={{0,16},{8,24},{16,0},{24,8},{1,17},{9,25},{17,1},{25,9},{2,18},{10... | collective-permute-start | bytes 1327112 | tf_op jit(solution)/shard_map/ppermute | solution.py:855
  258.1 13.0 %collective-permute-start.49 = (bf16[4,144,384]{2,1,0:T(8,128)(2,1)S(1)}, bf16[4,144,384]{2,1,0:T(8,128)(2,1)S(1)}, u32[]{:S(2)}, u32[]{:S(2)}) collective-permute-start(bf16[4,144,384]{2,1,0:T(8,128)(2,1)S(1)} %add_convert_fusion.1), channel_id=1, source_target_pairs={{0,8},{8,0},{16,24},{24,16},{1,9},{9,1},{17,25},{25,17},{2,10},{10... | collective-permute-start | bytes 1327112 | tf_op jit(solution)/shard_map/ppermute | solution.py:857
  259.4 15.0 %collective-permute-start.58 = (bf16[4,160,128]{2,1,0:T(8,128)(2,1)S(1)}, bf16[4,160,128]{2,1,0:T(8,128)(2,1)S(1)}, u32[]{:S(2)}, u32[]{:S(2)}) collective-permute-start(bf16[4,160,128]{2,1,0:T(8,128)(2,1)S(1)} %get-tuple-element.257), channel_id=1, source_target_pairs={{0,8},{8,0},{16,24},{24,16},{1,9},{9,1},{17,25},{25,17},{2,10},{10... | collective-permute-start | bytes 491528 | tf_op jit(solution)/shard_map/ppermute | solution.py:838
  267.0 10.3 %collective-permute-start.60 = (bf16[4,160,128]{2,1,0:T(8,128)(2,1)S(1)}, bf16[4,160,128]{2,1,0:T(8,128)(2,1)S(1)}, u32[]{:S(2)}, u32[]{:S(2)}) collective-permute-start(bf16[4,160,128]{2,1,0:T(8,128)(2,1)S(1)} %get-tuple-element.258), channel_id=1, source_target_pairs={{0,24},{8,16},{16,8},{24,0},{1,25},{9,17},{17,9},{25,1},{2,26},{10... | collective-permute-start | bytes 491528 | tf_op jit(solution)/shard_map/ppermute | solution.py:838
  278.6 10.7 %collective-permute-start.46 = (bf16[576,128]{1,0:T(8,128)(2,1)S(1)}, bf16[576,128]{1,0:T(8,128)(2,1)S(1)}, u32[]{:S(2)}, u32[]{:S(2)}) collective-permute-start(bf16[576,128]{1,0:T(8,128)(2,1)S(1)} %copy-done.64), channel_id=1, source_target_pairs={{0,4},{1,5},{2,6},{3,7},{4,0},{5,1},{6,2},{7,3},{8,12},{9,13},{10,... | collective-permute-start | bytes 442376 | tf_op jit(solution)/shard_map/ppermute | solution.py:930
  278.8 19.5 %collective-permute-start.47 = (bf16[576,128]{1,0:T(8,128)(2,1)S(1)}, bf16[576,128]{1,0:T(8,128)(2,1)S(1)}, u32[]{:S(2)}, u32[]{:S(2)}) collective-permute-start(bf16[576,128]{1,0:T(8,128)(2,1)S(1)} %copy-done.63), channel_id=1, source_target_pairs={{0,6},{1,7},{2,0},{3,1},{4,2},{5,3},{6,4},{7,5},{8,14},{9,15},{10,... | collective-permute-start | bytes 442376 | tf_op jit(solution)/shard_map/ppermute | solution.py:930
  281.4 16.8 %collective-permute-start.56 = (bf16[256,384]{1,0:T(8,128)(2,1)S(1)}, bf16[256,384]{1,0:T(8,128)(2,1)S(1)}, u32[]{:S(2)}, u32[]{:S(2)}) collective-permute-start(bf16[256,384]{1,0:T(8,128)(2,1)S(1)} %get-tuple-element.253), channel_id=1, source_target_pairs={{0,6},{1,7},{2,0},{3,1},{4,2},{5,3},{6,4},{7,5},{8,14},{9,15},{10,... | collective-permute-start | bytes 589832 | tf_op jit(solution)/shard_map/ppermute | solution.py:832
  283.2 28.5 %collective-permute-start.54 = (bf16[256,384]{1,0:T(8,128)(2,1)S(1)}, bf16[256,384]{1,0:T(8,128)(2,1)S(1)}, u32[]{:S(2)}, u32[]{:S(2)}) collective-permute-start(bf16[256,384]{1,0:T(8,128)(2,1)S(1)} %get-tuple-element.255), channel_id=1, source_target_pairs={{0,2},{1,3},{2,4},{3,5},{4,6},{5,7},{6,0},{7,1},{8,10},{9,11},{10,... | collective-permute-start | bytes 589832 | tf_op jit(solution)/shard_map/ppermute | solution.py:832
  285.9 25.8 %collective-permute-start.55 = (bf16[256,384]{1,0:T(8,128)(2,1)S(1)}, bf16[256,384]{1,0:T(8,128)(2,1)S(1)}, u32[]{:S(2)}, u32[]{:S(2)}) collective-permute-start(bf16[256,384]{1,0:T(8,128)(2,1)S(1)} %get-tuple-element.256), channel_id=1, source_target_pairs={{0,4},{1,5},{2,6},{3,7},{4,0},{5,1},{6,2},{7,3},{8,12},{9,13},{10,... | collective-permute-start | bytes 589832 | tf_op jit(solution)/shard_map/ppermute | solution.py:832
  289.3 22.4 %collective-permute-start.63 = (bf16[160,128]{1,0:T(8,128)(2,1)S(1)}, bf16[160,128]{1,0:T(8,128)(2,1)S(1)}, u32[]{:S(2)}, u32[]{:S(2)}) collective-permute-start(bf16[160,128]{1,0:T(8,128)(2,1)S(1)} %get-tuple-element.260), channel_id=1, source_target_pairs={{0,6},{1,7},{2,0},{3,1},{4,2},{5,3},{6,4},{7,5},{8,14},{9,15},{10,... | collective-permute-start | bytes 122888 | tf_op jit(solution)/shard_map/ppermute | solution.py:832
  298.2 13.7 %collective-permute-start.62 = (bf16[160,128]{1,0:T(8,128)(2,1)S(1)}, bf16[160,128]{1,0:T(8,128)(2,1)S(1)}, u32[]{:S(2)}, u32[]{:S(2)}) collective-permute-start(bf16[160,128]{1,0:T(8,128)(2,1)S(1)} %get-tuple-element.261), channel_id=1, source_target_pairs={{0,4},{1,5},{2,6},{3,7},{4,0},{5,1},{6,2},{7,3},{8,12},{9,13},{10,... | collective-permute-start | bytes 122888 | tf_op jit(solution)/shard_map/ppermute | solution.py:832
  298.3 13.7 %collective-permute-start.61 = (bf16[160,128]{1,0:T(8,128)(2,1)S(1)}, bf16[160,128]{1,0:T(8,128)(2,1)S(1)}, u32[]{:S(2)}, u32[]{:S(2)}) collective-permute-start(bf16[160,128]{1,0:T(8,128)(2,1)S(1)} %get-tuple-element.262), channel_id=1, source_target_pairs={{0,2},{1,3},{2,4},{3,5},{4,6},{5,7},{6,0},{7,1},{8,10},{9,11},{10,... | collective-permute-start | bytes 122888 | tf_op jit(solution)/shard_map/ppermute | solution.py:832
  (82 other events, 806.9 us)
where the time goes:
time: 322 us; the launch traced here: 315 us
  Pallas kernels  164 us (51%)
  starting transfers between devices  83.3 us (26%)
  waiting for transfers between devices  52.2 us (16%)
  local copies, waits for them, and re-layouts  7.23 us (2%)
  other arithmetic  6.42 us (2%)
    pallas_call x2, Pallas kernels, ffn_backward(): call(body, (steps,), ([SMEM_SPEC] if dealt else []) + [whole(x.shape) for...  36.3 us
    pallas_call x3, Pallas kernels, attend_backward(): call(body, (count,), [pl.BlockSpec((GRP, rows, 128), lambda j: (j + first...  30.5 us
    pallas_call x2, Pallas kernels, attend_forward(): call(body, (KV,), [pl.BlockSpec(memory_space=pltpu.SMEM), pl.BlockSpec((G...  21.2 us
    pallas_call x2, Pallas kernels, ffn_forward(): call(body, (steps,), ([SMEM_SPEC] if last else []) + [whole(h.shape), who...  21 us
    ppermute x12, starting transfers between devices, redeal(): lax.ppermute(pieces[d], 'ctx', shifted(ctx, group, d))  20.8 us
    ppermute x6, starting transfers between devices, sum_z(): lax.ppermute(mine[d], 'ctx', shifted(8, 2, d))  20.1 us
    ppermute x9, starting transfers between devices, spread_z(): return [x] + [lax.ppermute(x, 'ctx', shifted(8, 2, d)) for d in (1, 2, 3)]  15.3 us
    pallas_call x2, Pallas kernels, qkv_backward(): call(body, (1,), ([SMEM_SPEC] if final else []) + [whole(x.shape) for x i...  12 us
  transfers between devices with their start and end apart: 64, of which 18 were waited for; matrix products, arithmetic and copies ran while one was open for 2% of the time, Pallas kernels for 24%

commit v1 on v0

--- a/solution.py
+++ b/solution.py
@@ -835,8 +835,9 @@
 def sum_attn(pieces):
     keep, away = pieces[:4], pieces[4]
     back = lax.ppermute(away, "ctx", cross(1, 8))
-    moved = [lax.ppermute(total(keep[r], back[r]), "dp", cross(r, 4)) for r in (1, 2, 3)]
-    return sum_z(total(keep[0], back[0], *moved))
+    sums = [total(keep[r], back[r]) for r in (1, 2, 3)]
+    moved = [lax.ppermute(x, "dp", cross(r, 4)) for r, x in zip((1, 2, 3), sums)]
+    return sum_z(total(keep[0], back[0], *moved)), sums
 
 
 def sum_ffn(pieces):
@@ -856,8 +857,16 @@
     x_top, y_low = pair(1, top, top_far), pair(2, low, low_far)
     top_x = lax.ppermute(x_top, "dp", cross(1, 4))
     low_y = lax.ppermute(y_low, "dp", cross(2, 4))
-    mine = jnp.concatenate([pair(0, top, top_x, top_y), pair(0, low, low_x, low_y)], axis=1)
-    return sum_z(mine), (away, (far_top, far_low, x_low, y_top))
+    marks = (away, (far_top, far_low, x_low, y_top))
+
+    def along_z(mark):
+        moved = after((top_x, top_y, low_x, low_y), mark)
+        mine = jnp.concatenate(
+            [pair(0, top, moved[0], moved[1]), pair(0, low, moved[2], moved[3])], axis=1
+        )
+        return sum_z(mine)
+
+    return along_z, marks
 
 
 def finish(terms_f, terms_a):
@@ -1038,11 +1047,11 @@
             g, (h1, nb, a, b, hid, att), full, before_ffn, coords if layer == 1 else None
         )
         back_args = (q, kv_parts, datt, att, linv, probs, cs, sn, slots)
-        chunks = [(0, KV)] if layer == 1 else [(0, 1), (1, KV - 1)]
+        chunks = [(0, KV)]
         if layer == 0 and tight:
             grad_down, grad_gate, grad_up, grad_out, gn_ffn = before_ffn
             parts_f = split_ffn(coords, grad_out, grad_gate, grad_up, grad_down)
-            terms_f, marks = sum_ffn(parts_f)
+            along_z, marks = sum_ffn(parts_f)
         dq, sent = [], []
         for n, (first, count) in enumerate(chunks):
             args = back_args
@@ -1067,7 +1076,8 @@
     grad_down, grad_gate, grad_up, grad_out, gn_ffn = before_ffn
     if tight:
         split = split_attn(coords, d_qkv, na, before_qkv, gn_attn, gn_ffn)
-        done = finish(terms_f, sum_attn(split))
+        terms_a, sums_a = sum_attn(split)
+        done = finish(along_z(sums_a), terms_a)
         g_out, g_gate, g_up, g_down, g_query, g_key, g_value, gn_attn, gn_ffn = done
         g_key, g_value, g_down = g_key.T, g_value.T, g_down.T
         gn = (gn_attn[0], gn_ffn[0])

time: 322 us -> 330 us (1.025)
  waiting for transfers between devices: 52.2 us -> 58.1 us
    ppermute x1, waiting for transfers between devices: 0.01 us -> 14.2 us  [sum_ffn(): top_far = lax.ppermute(far_top, 'dp', cross(2, 4))]
    ppermute x1, waiting for transfers between devices: 0.01 us -> 6.22 us  [sum_ffn(): low_x = lax.ppermute(x_low, 'dp', cross(1, 4))]
    ppermute x1, waiting for transfers between devices: 5.73 us -> 0.01 us  [sum_ffn(): back = lax.ppermute(away, 'ctx', cross(1, 8))]
    ppermute x3, waiting for transfers between devices: 4.93 us -> 0.01 us  [sum_attn(): lax.ppermute(x, 'dp', cross(r, 4))]
    ppermute x6, starting transfers between devices: 20.1 us -> 23.7 us  [sum_z(): lax.ppermute(mine[d], 'ctx', shifted(8, 2, d))]
    ppermute x1, waiting for transfers between devices: 6.49 us -> 3.17 us  [sum_ffn(): top_y = lax.ppermute(y_top, 'dp', cross(2, 4))]
    pallas_call x3 -> x2, Pallas kernels: 30.5 us -> 27.6 us  [attend_backward(): call(body, (count,), [pl.BlockSpec((GRP, rows, 128), lambda j: (j + first...]
  transfers between devices with their start and end apart: 64 -> 63, of which waited for: 18 -> 17; matrix products, arithmetic and copies ran while one was open for 2% -> 3% of each run, Pallas kernels for 24% -> 23%
where the time goes in v1:
time: 330 us; the launch traced here: 323 us
  Pallas kernels  162 us (49%)
  starting transfers between devices  86.6 us (26%)
  waiting for transfers between devices  58.1 us (18%)
  other arithmetic  7.57 us (2%)
  local copies, waits for them, and re-layouts  7.32 us (2%)
    pallas_call x2, Pallas kernels, ffn_backward(): call(body, (steps,), ([SMEM_SPEC] if dealt else []) + [whole(x.shape) for...  36.3 us
    pallas_call x2, Pallas kernels, attend_backward(): call(body, (count,), [pl.BlockSpec((GRP, rows, 128), lambda j: (j + first...  27.6 us
    ppermute x6, starting transfers between devices, sum_z(): lax.ppermute(mine[d], 'ctx', shifted(8, 2, d))  23.7 us
    ppermute x12, starting transfers between devices, redeal(): lax.ppermute(pieces[d], 'ctx', shifted(ctx, group, d))  21.5 us
    pallas_call x2, Pallas kernels, attend_forward(): call(body, (KV,), [pl.BlockSpec(memory_space=pltpu.SMEM), pl.BlockSpec((G...  21.5 us
    pallas_call x2, Pallas kernels, ffn_forward(): call(body, (steps,), ([SMEM_SPEC] if last else []) + [whole(h.shape), who...  21 us
    ppermute x9, starting transfers between devices, spread_z(): return [x] + [lax.ppermute(x, 'ctx', shifted(8, 2, d)) for d in (1, 2, 3)]  15.4 us
    ppermute x1, waiting for transfers between devices, sum_ffn(): top_far = lax.ppermute(far_top, 'dp', cross(2, 4))  14.2 us
  transfers between devices with their start and end apart: 63, of which 17 were waited for; matrix products, arithmetic and copies ran while one was open for 3% of the time, Pallas kernels for 23%

profile of v1, /device:TPU:0, one launch (start us, length us, event | category | flops | bytes accessed | tf_op | source)
XLA Modules:
  0.0 323.2 jit_solution(5454354243471973832)
XLA Ops:
  0.7 1.9 shard_map.203
  2.5 5.1 %collective-permute-start.5 = (bf16[160,128]{1,0:T(8,128)(2,1)}, bf16[160,128]{1,0:T(8,128)(2,1)S(1)}, u32[]{:S(2)}, u32[]{:S(2)}) collective-permute-start(bf16[160,128]{1,0:T(8,128)(2,1)} %get-tuple-element.119), channel_id=1, source_target_pairs={{0,6},{1,7},{2,0},{3,1},{4,2},{5,3},{6,4},{7,5},{8,14},{9,15},{10,... | collective-permute-start | bytes 122888 | tf_op jit(solution)/shard_map/ppermute | solution.py:633
  8.7 2.8 collective-permute-start.22
  17.0 3.2 collective-permute-start.14
  20.2 2.5 collective-permute-start.8
  25.1 1.9 shard_map.204
  28.2 3.4 %collective-permute-start = (bf16[576,128]{1,0:T(8,128)(2,1)}, bf16[576,128]{1,0:T(8,128)(2,1)S(1)}, u32[]{:S(2)}, u32[]{:S(2)}) collective-permute-start(bf16[576,128]{1,0:T(8,128)(2,1)} %get-tuple-element.122), channel_id=1, source_target_pairs={{0,2},{1,3},{2,4},{3,5},{4,6},{5,7},{6,0},{7,1},{8,10},{9,11},{10,... | collective-permute-start | bytes 442376 | tf_op jit(solution)/shard_map/ppermute | solution.py:939
  31.6 1.6 collective-permute-start.1
  34.6 3.7 %collective-permute-start.2 = (bf16[576,128]{1,0:T(8,128)(2,1)}, bf16[576,128]{1,0:T(8,128)(2,1)S(1)}, u32[]{:S(2)}, u32[]{:S(2)}) collective-permute-start(bf16[576,128]{1,0:T(8,128)(2,1)} %get-tuple-element.124), channel_id=1, source_target_pairs={{0,6},{1,7},{2,0},{3,1},{4,2},{5,3},{6,4},{7,5},{8,14},{9,15},{10,... | collective-permute-start | bytes 442376 | tf_op jit(solution)/shard_map/ppermute | solution.py:939
  38.4 3.7 %collective-permute-done.20 = bf16[112,384]{1,0:T(8,128)(2,1)S(1)} collective-permute-done((bf16[112,384]{1,0:T(8,128)(2,1)S(1)}, bf16[112,384]{1,0:T(8,128)(2,1)S(1)}, u32[]{:S(2)}, u32[]{:S(2)}) %collective-permute-start.20) | collective-permute-done | bytes 86048 | tf_op jit(solution)/shard_map/ppermute | solution.py:633
  49.2 3.3 %collective-permute-done.17.refs_1_ = bf16[4,144,384]{2,1,0:T(8,128)(2,1)S(1)} collective-permute-done((bf16[4,144,384]{2,1,0:T(8,128)(2,1)S(1)}, bf16[4,144,384]{2,1,0:T(8,128)(2,1)S(1)}, u32[]{:S(2)}, u32[]{:S(2)}) %collective-permute-start.17) | collective-permute-done | bytes 442400 | tf_op jit(solution)/shard_map/ppermute | solution.py:645
  52.5 2.1 collective-permute-start.19
  54.7 3.4 %shard_map.205 = (bf16[576,960]{1,0:T(8,128)(2,1)}, f32[16,576]{1,0:T(8,128)}) custom-call(s32[3]{0:T(128)} %pad_add_fusion.co.refs_0_, bf16[4,160,128]{2,1,0:T(8,128)(2,1)} %copy-done.10, bf16[4,160,128]{2,1,0:T(8,128)(2,1)} %copy-done.32, bf16[4,160,128]{2,1,0:T(8,128)(2,1)} %copy-done.31, bf16[4,160,128]{2,1,0:T(8,128)(2,1)} %copy-done.30, ...), custom_call_target="tpu_custom_call" | custom-call | tf_op jit(solution)/shard_map/pallas_call | solution.py:681
  58.0 4.7 %shard_map.206 = (bf16[512,576]{1,0:T(8,128)(2,1)}, bf16[9,512,128]{2,1,0:T(8,128)(2,1)}, bf16[3,512,128]{2,1,0:T(8,128)(2,1)}, f32[512,576]{1,0:T(8,128)}) custom-call(s32[3]{0:T(128)} %pad_add_fusion.co.refs_0_, bf16[576,128]{1,0:T(8,128)(2,1)} %get-tuple-element.121.refs_1_, bf16[576,128]{1,0:T(8,128)(2,1)} %copy-done.38, bf16[576,128]{1,0:T(8,128)(2,1)} %copy-done.39, ...), custom_call_target="tpu_custom_call" | custom-call | tf_op jit(solution)/shard_map/pallas_call | solution.py:115
  66.1 8.0 %collective-permute-done.19.refs_3_ = bf16[4,144,384]{2,1,0:T(8,128)(2,1)S(1)} collective-permute-done((bf16[4,144,384]{2,1,0:T(8,128)(2,1)S(1)}, bf16[4,144,384]{2,1,0:T(8,128)(2,1)S(1)}, u32[]{:S(2)}, u32[]{:S(2)}) %collective-permute-start.19) | collective-permute-done | bytes 442400 | tf_op jit(solution)/shard_map/ppermute | solution.py:649
  74.7 10.9 %shard_map.207 = (bf16[3,512,192]{2,1,0:T(8,128)(2,1)}, f32[3,512,128]{2,1,0:T(8,128)}, bf16[3,512,384]{2,1,0:T(8,128)(2,1)}, bf16[3,512,384]{2,1,0:T(8,128)(2,1...) custom-call(s32[3]{0:T(128)} %pad_add_fusion.1.meta_ref, bf16[9,512,128]{2,1,0:T(8,128)(2,1)} %get-tuple-element.184.q_ref, ...), custom_call_target="tpu_custom_call" | custom-call | tf_op jit(solution)/shard_map/pallas_call | solution.py:200
  87.6 6.3 %shard_map.208 = (bf16[576,576]{1,0:T(8,128)(2,1)}, bf16[576,1536]{1,0:T(8,128)(2,1)}, bf16[576,1536]{1,0:T(8,128)(2,1)}, bf16[576,1536]{1,0:T(8,128)(2,1)}) custom-call(s32[3]{0:T(128)} %pad_add_fusion.co.refs_0_, bf16[4,144,384]{2,1,0:T(8,128)(2,1)} %copy-done.2, bf16[4,144,384]{2,1,0:T(8,128)(2,1)} %copy-done.11, bf16[4,144,384]{2,1,0:T(8,128)(2,1)} %copy-done.13, ...), custom_call_target="tpu_custom_call" | custom-call | tf_op jit(solution)/shard_map/pallas_call | solution.py:729
  93.9 9.8 %shard_map.209 = (f32[512,576]{1,0:T(8,128)}, bf16[512,576]{1,0:T(8,128)(2,1)}, bf16[512,1536]{1,0:T(8,128)(2,1)}, bf16[512,1536]{1,0:T(8,128)(2,1)}, bf16[512,1536]{1,0:T(8,128)(2,1)}, /*index=5*/f32[512,576]{1,0:T(8,128)}) custom-call(f32[512,576]{1,0:T(8,128)} %get-tuple-element.130.refs_0_.refs_5_, ...), custom_call_target="tpu_custom_call" | custom-call | tf_op jit(solution)/shard_map/pallas_call | solution.py:360
  103.7 4.5 %shard_map.210 = (bf16[512,576]{1,0:T(8,128)(2,1)}, bf16[9,512,128]{2,1,0:T(8,128)(2,1)}, bf16[3,512,128]{2,1,0:T(8,128)(2,1)}) custom-call(f32[512,576]{1,0:T(8,128)} %get-tuple-element.140.refs_0_.refs_1_.refs_4_, f32[16,576]{1,0:T(8,128)} %get-tuple-element.128.refs_5_.refs_3_.refs_1_.refs_4_.refs_11_.refs_6_.refs_7_, ...), custom_call_target="tpu_custom_call" | custom-call | tf_op jit(solution)/shard_map/pallas_call | solution.py:115
  108.6 2.0 shard_map.214
  110.6 4.0 %collective-permute-start.38 = (bf16[576,128]{1,0:T(8,128)(2,1)}, bf16[576,128]{1,0:T(8,128)(2,1)S(1)}, u32[]{:S(2)}, u32[]{:S(2)}) collective-permute-start(bf16[576,128]{1,0:T(8,128)(2,1)} %get-tuple-element.149), channel_id=1, source_target_pairs={{0,2},{1,3},{2,4},{3,5},{4,6},{5,7},{6,0},{7,1},{8,10},{9,11},{10,... | collective-permute-start | bytes 442376 | tf_op jit(solution)/shard_map/ppermute | solution.py:939
  114.7 1.9 collective-permute-start.39
  116.6 2.9 collective-permute-start.40
  120.3 10.5 %shard_map.211 = (bf16[3,512,192]{2,1,0:T(8,128)(2,1)}, f32[3,512,128]{2,1,0:T(8,128)}, bf16[3,512,384]{2,1,0:T(8,128)(2,1)}, bf16[3,512,384]{2,1,0:T(8,128)(2,1...) custom-call(s32[3]{0:T(128)} %pad_add_fusion.1.meta_ref, bf16[9,512,128]{2,1,0:T(8,128)(2,1)} %get-tuple-element.141.q_ref, ...), custom_call_target="tpu_custom_call" | custom-call | tf_op jit(solution)/shard_map/pallas_call | solution.py:200
  130.8 11.2 %shard_map.212 = (f32[512,576]{1,0:T(8,128)}, bf16[512,576]{1,0:T(8,128)(2,1)}, bf16[512,1536]{1,0:T(8,128)(2,1)}, bf16[512,1536]{1,0:T(8,128)(2,1)}, bf16[512,1...) custom-call(s32[3]{0:T(128)} %pad_add_fusion.co.refs_0_, ...), custom_call_target="tpu_custom_call" | custom-call | tf_op jit(solution)/shard_map/pallas_call | solution.py:360
  142.8 17.1 %shard_map.215 = (f32[576,1536]{1,0:T(8,128)}, f32[576,1536]{1,0:T(8,128)}, f32[576,1536]{1,0:T(8,128)}, f32[576,576]{1,0:T(8,128)}, f32[1,576]{1,0:T(1,128)}, /...) custom-call(s32[3]{0:T(128)} %pad_add_fusion.co.refs_0_, bf16[576,128]{1,0:T(8,128)(2,1)} %get-tuple-element.148.refs_1_, ...), custom_call_target="tpu_custom_call" | custom-call | tf_op jit(solution)/shard_map/pallas_call | solution.py:459
  159.9 13.8 %shard_map.216 = (bf16[3,512,192]{2,1,0:T(8,128)(2,1)}, bf16[3,512,128]{2,1,0:T(8,128)(2,1)}, bf16[3,512,128]{2,1,0:T(8,128)(2,1)}) custom-call(bf16[9,512,128]{2,1,0:T(8,128)(2,1)} %get-tuple-element.141.q_ref, bf16[3,512,192]{2,1,0:T(8,128)(2,1)} %get-tuple-element.157.datt_ref, bf16[3,512,192]{2,1,0:T(8,128)(2,1)} %get-tuple-element.143.refs_2_.refs_10_.att_ref, ...), custom_call_target="tpu_custom_call" | custom-call | tf_op jit(solution)/shard_map/pallas_call | solution.py:284
  173.8 1.9 collective-permute-done.41.refs_2_
  176.4 6.6 %shard_map.217 = (f32[576,960]{1,0:T(8,128)}, f32[1,576]{1,0:T(1,128)}, f32[512,576]{1,0:T(8,128)}) custom-call(bf16[3,512,192]{2,1,0:T(8,128)(2,1)} %get-tuple-element.163.refs_0_, bf16[3,512,128]{2,1,0:T(8,128)(2,1)} %get-tuple-element.164.refs_1_, bf16[3,512,128]{2,1,0:T(8,128)(2,1)} %copy-done.19, bf16[512,576]{1,0:T(8,128)(2,1)} %get-tuple-element.166.refs_3_, ...), custom_call_target="tpu_custom_call" | custom-call | tf_op jit(solution)/shard_map/pallas_call | solution.py:547
  183.0 19.2 %shard_map.218 = (bf16[576,1536]{1,0:T(8,128)(2,1)}, bf16[576,1536]{1,0:T(8,128)(2,1)}, bf16[576,1536]{1,0:T(8,128)(2,1)}, bf16[576,576]{1,0:T(8,128)(2,1)}, f32...) custom-call(f32[512,576]{1,0:T(8,128)} %get-tuple-element.168.refs_0_, ...), custom_call_target="tpu_custom_call" | custom-call | tf_op jit(solution)/shard_map/pallas_call | solution.py:459
  202.2 6.7 %shard_map.219 = (bf16[4,256,384]{2,1,0:T(8,128)(2,1)}, bf16[4,256,384]{2,1,0:T(8,128)(2,1)}, bf16[4,256,384]{2,1,0:T(8,128)(2,1)}, bf16[4,256,384]{2,1,0:T(8,128)(2,1)}, bf16[4,4,256,384]{3,2,1,0:T(8,128)(2,1)}) custom-call(s32[3]{0:T(128)} %pad_add_fusion.co.refs_0_, bf16[576,576]{1,0:T(8,128)(2,1)} %get-tuple-element.179.go, ...), custom_call_target="tpu_custom_call" | custom-call | tf_op jit(solution)/shard_map/pallas_call | solution.py:815
  209.1 13.8 %shard_map.220 = (bf16[3,512,192]{2,1,0:T(8,128)(2,1)}, bf16[3,512,128]{2,1,0:T(8,128)(2,1)}, bf16[3,512,128]{2,1,0:T(8,128)(2,1)}) custom-call(bf16[9,512,128]{2,1,0:T(8,128)(2,1)} %get-tuple-element.184.q_ref, bf16[3,512,192]{2,1,0:T(8,128)(2,1)} %get-tuple-element.185.datt_ref, bf16[3,512,192]{2,1,0:T(8,128)(2,1)} %get-tuple-element.133.refs_1_.refs_6_.att_ref, ...), custom_call_target="tpu_custom_call" | custom-call | tf_op jit(solution)/shard_map/pallas_call | solution.py:284
  225.7 5.7 %shard_map.221 = (bf16[512,960]{1,0:T(8,128)(2,1)}, f32[1,576]{1,0:T(1,128)}, bf16[576,128]{1,0:T(8,128)(2,1)}, bf16[576,128]{1,0:T(8,128)(2,1)}, bf16[576,128]{1,0:T(8,128)(2,1)}, /*index=5*/bf16[576,128]{1,0:T(8,128)(2,1)}) custom-call(s32[3]{0:T(128)} %pad_add_fusion.co.refs_0_, bf16[3,512,192]{2,1,0:T(8,128)(2,1)} %get-tuple-element.191.refs_1_, ...), custom_call_target="tpu_custom_call" | custom-call | tf_op jit(solution)/shard_map/pallas_call | solution.py:547
  231.4 5.1 %shard_map.223 = (bf16[4,160,128]{2,1,0:T(8,128)(2,1)}, bf16[4,160,128]{2,1,0:T(8,128)(2,1)}, bf16[4,160,128]{2,1,0:T(8,128)(2,1)}, bf16[4,160,128]{2,1,0:T(8,128)(2,1)}, bf16[4,4,160,128]{3,2,1,0:T(8,128)(2,1)}) custom-call(s32[3]{0:T(128)} %pad_add_fusion.co.refs_0_, bf16[512,960]{1,0:T(8,128)(2,1)} %get-tuple-element.205.d_ref, ...), custom_call_target="tpu_custom_call" | custom-call | tf_op jit(solution)/shard_map/pallas_call | solution.py:771
  236.9 1.9 collective-permute-done.53
  246.0 14.2 %collective-permute-done.47 = bf16[4,144,384]{2,1,0:T(8,128)(2,1)S(1)} collective-permute-done((bf16[4,144,384]{2,1,0:T(8,128)(2,1)S(1)}, bf16[4,144,384]{2,1,0:T(8,128)(2,1)S(1)}, u32[]{:S(2)}, u32[]{:S(2)}) %collective-permute-start.47) | collective-permute-done | bytes 442400 | tf_op jit(solution)/shard_map/ppermute | solution.py:853
  263.2 1.7 collective-permute-start.52
  265.0 6.2 %collective-permute-done.50 = bf16[4,112,384]{2,1,0:T(8,128)(2,1)S(1)} collective-permute-done((bf16[4,112,384]{2,1,0:T(8,128)(2,1)S(1)}, bf16[4,112,384]{2,1,0:T(8,128)(2,1)S(1)}, u32[]{:S(2)}, u32[]{:S(2)}) %collective-permute-start.50) | collective-permute-done | bytes 344096 | tf_op jit(solution)/shard_map/ppermute | solution.py:855
  271.2 3.2 collective-permute-done.49
  274.4 5.6 %collective-permute-done.52 = bf16[4,112,384]{2,1,0:T(8,128)(2,1)S(1)} collective-permute-done((bf16[4,112,384]{2,1,0:T(8,128)(2,1)S(1)}, bf16[4,112,384]{2,1,0:T(8,128)(2,1)S(1)}, u32[]{:S(2)}, u32[]{:S(2)}) %collective-permute-start.52) | collective-permute-done | bytes 344096 | tf_op jit(solution)/shard_map/ppermute | solution.py:859
  281.9 3.3 %collective-permute-start.45 = (bf16[576,128]{1,0:T(8,128)(2,1)S(1)}, bf16[576,128]{1,0:T(8,128)(2,1)S(1)}, u32[]{:S(2)}, u32[]{:S(2)}) collective-permute-start(bf16[576,128]{1,0:T(8,128)(2,1)S(1)} %copy-done.59), channel_id=1, source_target_pairs={{0,6},{1,7},{2,0},{3,1},{4,2},{5,3},{6,4},{7,5},{8,14},{9,15},{10,... | collective-permute-start | bytes 442376 | tf_op jit(solution)/shard_map/ppermute | solution.py:939
  289.9 2.6 collective-permute-done.44.refs_2_
  292.5 8.4 %collective-permute-start.62 = (bf16[160,128]{1,0:T(8,128)(2,1)S(1)}, bf16[160,128]{1,0:T(8,128)(2,1)S(1)}, u32[]{:S(2)}, u32[]{:S(2)}) collective-permute-start(bf16[160,128]{1,0:T(8,128)(2,1)S(1)} %get-tuple-element.260), channel_id=1, source_target_pairs={{0,6},{1,7},{2,0},{3,1},{4,2},{5,3},{6,4},{7,5},{8,14},{9,15},{10,... | collective-permute-start | bytes 122888 | tf_op jit(solution)/shard_map/ppermute | solution.py:832
  300.9 1.7 collective-permute-done.62.refs_7_
  302.6 12.7 %collective-permute-start.60 = (bf16[160,128]{1,0:T(8,128)(2,1)S(1)}, bf16[160,128]{1,0:T(8,128)(2,1)S(1)}, u32[]{:S(2)}, u32[]{:S(2)}) collective-permute-start(bf16[160,128]{1,0:T(8,128)(2,1)S(1)} %get-tuple-element.262), channel_id=1, source_target_pairs={{0,2},{1,3},{2,4},{3,5},{4,6},{5,7},{6,0},{7,1},{8,10},{9,11},{10,... | collective-permute-start | bytes 122888 | tf_op jit(solution)/shard_map/ppermute | solution.py:832
  315.2 2.0 shard_map.213
  317.3 2.2 shard_map.222
  320.4 2.4 shard_map.224
  (249 shorter events, 47.7 us)
Async XLA Ops:
  2.5 12.5 %collective-permute-start.5 = (bf16[160,128]{1,0:T(8,128)(2,1)}, bf16[160,128]{1,0:T(8,128)(2,1)S(1)}, u32[]{:S(2)}, u32[]{:S(2)}) collective-permute-start(bf16[160,128]{1,0:T(8,128)(2,1)} %get-tuple-element.119), channel_id=1, source_target_pairs={{0,6},{1,7},{2,0},{3,1},{4,2},{5,3},{6,4},{7,5},{8,14},{9,15},{10,... | collective-permute-start | bytes 122888 | tf_op jit(solution)/shard_map/ppermute | solution.py:633
  8.7 11.5 %collective-permute-start.22 = (bf16[112,384]{1,0:T(8,128)(2,1)}, bf16[112,384]{1,0:T(8,128)(2,1)S(1)}, u32[]{:S(2)}, u32[]{:S(2)}) collective-permute-start(bf16[112,384]{1,0:T(8,128)(2,1)} %get-tuple-element.135), channel_id=1, source_target_pairs={{0,6},{1,7},{2,0},{3,1},{4,2},{5,3},{6,4},{7,5},{8,14},{9,15},{10,... | collective-permute-start | bytes 258056 | tf_op jit(solution)/shard_map/ppermute | solution.py:633
  11.5 11.2 %collective-permute-start.21 = (bf16[112,384]{1,0:T(8,128)(2,1)}, bf16[112,384]{1,0:T(8,128)(2,1)S(1)}, u32[]{:S(2)}, u32[]{:S(2)}) collective-permute-start(bf16[112,384]{1,0:T(8,128)(2,1)} %get-tuple-element.135), channel_id=1, source_target_pairs={{0,4},{1,5},{2,6},{3,7},{4,0},{5,1},{6,2},{7,3},{8,12},{9,13},{10,... | collective-permute-start | bytes 258056 | tf_op jit(solution)/shard_map/ppermute | solution.py:633
  16.0 12.3 %collective-permute-start.15 = (bf16[144,384]{1,0:T(8,128)(2,1)S(1)}, bf16[144,384]{1,0:T(8,128)(2,1)S(1)}, u32[]{:S(2)}, u32[]{:S(2)}) collective-permute-start(bf16[144,384]{1,0:T(8,128)(2,1)S(1)} %copy-done.50), channel_id=1, source_target_pairs={{0,4},{1,5},{2,6},{3,7},{4,0},{5,1},{6,2},{7,3},{8,12},{9,13},{10,... | collective-permute-start | bytes 331784 | tf_op jit(solution)/shard_map/ppermute | solution.py:633
  17.0 14.7 %collective-permute-start.14 = (bf16[144,384]{1,0:T(8,128)(2,1)S(1)}, bf16[144,384]{1,0:T(8,128)(2,1)S(1)}, u32[]{:S(2)}, u32[]{:S(2)}) collective-permute-start(bf16[144,384]{1,0:T(8,128)(2,1)S(1)} %copy-done.50), channel_id=1, source_target_pairs={{0,2},{1,3},{2,4},{3,5},{4,6},{5,7},{6,0},{7,1},{8,10},{9,11},{10,... | collective-permute-start | bytes 331784 | tf_op jit(solution)/shard_map/ppermute | solution.py:633
  20.2 14.2 %collective-permute-start.8 = (bf16[4,160,128]{2,1,0:T(8,128)(2,1)S(1)}, bf16[4,160,128]{2,1,0:T(8,128)(2,1)S(1)}, u32[]{:S(2)}, u32[]{:S(2)}) collective-permute-start(bf16[4,160,128]{2,1,0:T(8,128)(2,1)S(1)} %pad_maximum_fusion.5.refs_0_), channel_id=1, source_target_pairs={{0,24},{8,16},{16,8},{24,0},{1,25},{9,17},{17,9},{25,1},{2,26},{10... | collective-permute-start | bytes 491528 | tf_op jit(solution)/shard_map/ppermute | solution.py:638
  22.7 11.8 %collective-permute-start.7 = (bf16[4,160,128]{2,1,0:T(8,128)(2,1)S(1)}, bf16[4,160,128]{2,1,0:T(8,128)(2,1)S(1)}, u32[]{:S(2)}, u32[]{:S(2)}) collective-permute-start(bf16[4,160,128]{2,1,0:T(8,128)(2,1)S(1)} %pad_maximum_fusion.5.refs_0_), channel_id=1, source_target_pairs={{0,16},{8,24},{16,0},{24,8},{1,17},{9,25},{17,1},{25,9},{2,18},{10... | collective-permute-start | bytes 491528 | tf_op jit(solution)/shard_map/ppermute | solution.py:638
  23.2 15.1 %collective-permute-start.6 = (bf16[4,160,128]{2,1,0:T(8,128)(2,1)S(1)}, bf16[4,160,128]{2,1,0:T(8,128)(2,1)S(1)}, u32[]{:S(2)}, u32[]{:S(2)}) collective-permute-start(bf16[4,160,128]{2,1,0:T(8,128)(2,1)S(1)} %pad_maximum_fusion.5.refs_0_), channel_id=1, source_target_pairs={{0,8},{8,0},{16,24},{24,16},{1,9},{9,1},{17,25},{25,17},{2,10},{10... | collective-permute-start | bytes 491528 | tf_op jit(solution)/shard_map/ppermute | solution.py:638
  28.2 15.3 %collective-permute-start = (bf16[576,128]{1,0:T(8,128)(2,1)}, bf16[576,128]{1,0:T(8,128)(2,1)S(1)}, u32[]{:S(2)}, u32[]{:S(2)}) collective-permute-start(bf16[576,128]{1,0:T(8,128)(2,1)} %get-tuple-element.122), channel_id=1, source_target_pairs={{0,2},{1,3},{2,4},{3,5},{4,6},{5,7},{6,0},{7,1},{8,10},{9,11},{10,... | collective-permute-start | bytes 442376 | tf_op jit(solution)/shard_map/ppermute | solution.py:939
  31.6 12.1 %collective-permute-start.1 = (bf16[576,128]{1,0:T(8,128)(2,1)}, bf16[576,128]{1,0:T(8,128)(2,1)S(1)}, u32[]{:S(2)}, u32[]{:S(2)}) collective-permute-start(bf16[576,128]{1,0:T(8,128)(2,1)} %get-tuple-element.123), channel_id=1, source_target_pairs={{0,4},{1,5},{2,6},{3,7},{4,0},{5,1},{6,2},{7,3},{8,12},{9,13},{10,... | collective-permute-start | bytes 442376 | tf_op jit(solution)/shard_map/ppermute | solution.py:939
  42.1 10.4 %collective-permute-start.17 = (bf16[4,144,384]{2,1,0:T(8,128)(2,1)S(1)}, bf16[4,144,384]{2,1,0:T(8,128)(2,1)S(1)}, u32[]{:S(2)}, u32[]{:S(2)}) collective-permute-start(bf16[4,144,384]{2,1,0:T(8,128)(2,1)S(1)} %pad_maximum_fusion.refs_0_), channel_id=1, source_target_pairs={{0,8},{8,0},{16,24},{24,16},{1,9},{9,1},{17,25},{25,17},{2,10},{10... | collective-permute-start | bytes 1327112 | tf_op jit(solution)/shard_map/ppermute | solution.py:645
  45.1 17.6 %collective-permute-start.24 = (bf16[4,112,384]{2,1,0:T(8,128)(2,1)S(1)}, bf16[4,112,384]{2,1,0:T(8,128)(2,1)S(1)}, u32[]{:S(2)}, u32[]{:S(2)}) collective-permute-start(bf16[4,112,384]{2,1,0:T(8,128)(2,1)S(1)} %pad_maximum_fusion.1.refs_4_), channel_id=1, source_target_pairs={{0,16},{8,24},{16,0},{24,8},{1,17},{9,25},{17,1},{25,9},{2,18},{10... | collective-permute-start | bytes 1032200 | tf_op jit(solution)/shard_map/ppermute | solution.py:646
  46.5 16.8 %collective-permute-start.26 = (bf16[4,144,384]{2,1,0:T(8,128)(2,1)S(1)}, bf16[4,144,384]{2,1,0:T(8,128)(2,1)S(1)}, u32[]{:S(2)}, u32[]{:S(2)}) collective-permute-start(bf16[4,144,384]{2,1,0:T(8,128)(2,1)S(1)} %pad_maximum_fusion.refs_0_), channel_id=1, source_target_pairs={{0,1},{1,0},{2,3},{3,2},{4,5},{5,4},{6,7},{7,6},{8,9},{9,8},{10,11... | collective-permute-start | bytes 1327112 | tf_op jit(solution)/shard_map/ppermute | solution.py:652
  46.5 16.3 %collective-permute-start.23 = (bf16[4,112,384]{2,1,0:T(8,128)(2,1)S(1)}, bf16[4,112,384]{2,1,0:T(8,128)(2,1)S(1)}, u32[]{:S(2)}, u32[]{:S(2)}) collective-permute-start(bf16[4,112,384]{2,1,0:T(8,128)(2,1)S(1)} %pad_maximum_fusion.1.refs_4_), channel_id=1, source_target_pairs={{0,8},{8,0},{16,24},{24,16},{1,9},{9,1},{17,25},{25,17},{2,10},{10... | collective-permute-start | bytes 1032200 | tf_op jit(solution)/shard_map/ppermute | solution.py:648
  47.9 17.6 %collective-permute-start.18 = (bf16[4,144,384]{2,1,0:T(8,128)(2,1)S(1)}, bf16[4,144,384]{2,1,0:T(8,128)(2,1)S(1)}, u32[]{:S(2)}, u32[]{:S(2)}) collective-permute-start(bf16[4,144,384]{2,1,0:T(8,128)(2,1)S(1)} %pad_maximum_fusion.refs_0_), channel_id=1, source_target_pairs={{0,16},{8,24},{16,0},{24,8},{1,17},{9,25},{17,1},{25,9},{2,18},{10... | collective-permute-start | bytes 1327112 | tf_op jit(solution)/shard_map/ppermute | solution.py:647
  52.5 21.6 %collective-permute-start.19 = (bf16[4,144,384]{2,1,0:T(8,128)(2,1)S(1)}, bf16[4,144,384]{2,1,0:T(8,128)(2,1)S(1)}, u32[]{:S(2)}, u32[]{:S(2)}) collective-permute-start(bf16[4,144,384]{2,1,0:T(8,128)(2,1)S(1)} %collective-permute-done.17.refs_1_), channel_id=1, source_target_pairs={{0,16},{8,24},{16,0},{24,8},{1,17},{9,25},{17,1},{25,9},{2,18},{10... | collective-permute-start | bytes 1327112 | tf_op jit(solution)/shard_map/ppermute | solution.py:649
  62.8 11.3 %collective-permute-start.32 = (bf16[4,112,384]{2,1,0:T(8,128)(2,1)S(1)}, bf16[4,112,384]{2,1,0:T(8,128)(2,1)S(1)}, u32[]{:S(2)}, u32[]{:S(2)}) collective-permute-start(bf16[4,112,384]{2,1,0:T(8,128)(2,1)S(1)} %collective-permute-done.24.refs_6_), channel_id=1, source_target_pairs={{0,1},{1,0},{2,3},{3,2},{4,5},{5,4},{6,7},{7,6},{8,9},{9,8},{10,11... | collective-permute-start | bytes 1032200 | tf_op jit(solution)/shard_map/ppermute | solution.py:652
  63.3 11.3 %collective-permute-start.25 = (bf16[4,112,384]{2,1,0:T(8,128)(2,1)S(1)}, bf16[4,112,384]{2,1,0:T(8,128)(2,1)S(1)}, u32[]{:S(2)}, u32[]{:S(2)}) collective-permute-start(bf16[4,112,384]{2,1,0:T(8,128)(2,1)S(1)} %collective-permute-done.24.refs_6_), channel_id=1, source_target_pairs={{0,8},{8,0},{16,24},{24,16},{1,9},{9,1},{17,25},{25,17},{2,10},{10... | collective-permute-start | bytes 1032200 | tf_op jit(solution)/shard_map/ppermute | solution.py:650
  65.5 20.1 %collective-permute-start.28 = (bf16[4,144,384]{2,1,0:T(8,128)(2,1)S(1)}, bf16[4,144,384]{2,1,0:T(8,128)(2,1)S(1)}, u32[]{:S(2)}, u32[]{:S(2)}) collective-permute-start(bf16[4,144,384]{2,1,0:T(8,128)(2,1)S(1)} %collective-permute-done.18.refs_2_), channel_id=1, source_target_pairs={{0,1},{1,0},{2,3},{3,2},{4,5},{5,4},{6,7},{7,6},{8,9},{9,8},{10,11... | collective-permute-start | bytes 1327112 | tf_op jit(solution)/shard_map/ppermute | solution.py:652
  65.5 20.1 %collective-permute-start.27 = (bf16[4,144,384]{2,1,0:T(8,128)(2,1)S(1)}, bf16[4,144,384]{2,1,0:T(8,128)(2,1)S(1)}, u32[]{:S(2)}, u32[]{:S(2)}) collective-permute-start(bf16[4,144,384]{2,1,0:T(8,128)(2,1)S(1)} %collective-permute-done.17.refs_1_), channel_id=1, source_target_pairs={{0,1},{1,0},{2,3},{3,2},{4,5},{5,4},{6,7},{7,6},{8,9},{9,8},{10,11... | collective-permute-start | bytes 1327112 | tf_op jit(solution)/shard_map/ppermute | solution.py:652
  74.1 11.6 %collective-permute-start.29 = (bf16[4,144,384]{2,1,0:T(8,128)(2,1)S(1)}, bf16[4,144,384]{2,1,0:T(8,128)(2,1)S(1)}, u32[]{:S(2)}, u32[]{:S(2)}) collective-permute-start(bf16[4,144,384]{2,1,0:T(8,128)(2,1)S(1)} %collective-permute-done.19.refs_3_), channel_id=1, source_target_pairs={{0,1},{1,0},{2,3},{3,2},{4,5},{5,4},{6,7},{7,6},{8,9},{9,8},{10,11... | collective-permute-start | bytes 1327112 | tf_op jit(solution)/shard_map/ppermute | solution.py:652
  74.1 11.5 %collective-permute-start.31 = (bf16[4,112,384]{2,1,0:T(8,128)(2,1)S(1)}, bf16[4,112,384]{2,1,0:T(8,128)(2,1)S(1)}, u32[]{:S(2)}, u32[]{:S(2)}) collective-permute-start(bf16[4,112,384]{2,1,0:T(8,128)(2,1)S(1)} %collective-permute-done.23.refs_5_), channel_id=1, source_target_pairs={{0,1},{1,0},{2,3},{3,2},{4,5},{5,4},{6,7},{7,6},{8,9},{9,8},{10,11... | collective-permute-start | bytes 1032200 | tf_op jit(solution)/shard_map/ppermute | solution.py:652
  74.6 11.1 %collective-permute-start.33 = (bf16[4,112,384]{2,1,0:T(8,128)(2,1)S(1)}, bf16[4,112,384]{2,1,0:T(8,128)(2,1)S(1)}, u32[]{:S(2)}, u32[]{:S(2)}) collective-permute-start(bf16[4,112,384]{2,1,0:T(8,128)(2,1)S(1)} %collective-permute-done.25.refs_7_), channel_id=1, source_target_pairs={{0,1},{1,0},{2,3},{3,2},{4,5},{5,4},{6,7},{7,6},{8,9},{9,8},{10,11... | collective-permute-start | bytes 1032200 | tf_op jit(solution)/shard_map/ppermute | solution.py:652
  108.2 11.3 %collective-permute-start.34 = (bf16[3,512,128]{2,1,0:T(8,128)(2,1)}, bf16[3,512,128]{2,1,0:T(8,128)(2,1)S(1)}, u32[]{:S(2)}, u32[]{:S(2)}) collective-permute-start(bf16[3,512,128]{2,1,0:T(8,128)(2,1)} %get-tuple-element.142.refs_0_), channel_id=1, source_target_pairs={{0,1},{1,0},{2,3},{3,2},{4,5},{5,4},{6,7},{7,6},{8,9},{9,8},{10,11... | collective-permute-start | bytes 1179656 | tf_op jit(solution)/shard_map/ppermute | solution.py:945
  110.6 31.4 %collective-permute-start.38 = (bf16[576,128]{1,0:T(8,128)(2,1)}, bf16[576,128]{1,0:T(8,128)(2,1)S(1)}, u32[]{:S(2)}, u32[]{:S(2)}) collective-permute-start(bf16[576,128]{1,0:T(8,128)(2,1)} %get-tuple-element.149), channel_id=1, source_target_pairs={{0,2},{1,3},{2,4},{3,5},{4,6},{5,7},{6,0},{7,1},{8,10},{9,11},{10,... | collective-permute-start | bytes 442376 | tf_op jit(solution)/shard_map/ppermute | solution.py:939
  114.7 27.4 %collective-permute-start.39 = (bf16[576,128]{1,0:T(8,128)(2,1)}, bf16[576,128]{1,0:T(8,128)(2,1)S(1)}, u32[]{:S(2)}, u32[]{:S(2)}) collective-permute-start(bf16[576,128]{1,0:T(8,128)(2,1)} %get-tuple-element.150), channel_id=1, source_target_pairs={{0,4},{1,5},{2,6},{3,7},{4,0},{5,1},{6,2},{7,3},{8,12},{9,13},{10,... | collective-permute-start | bytes 442376 | tf_op jit(solution)/shard_map/ppermute | solution.py:939
  116.6 25.5 %collective-permute-start.40 = (bf16[576,128]{1,0:T(8,128)(2,1)}, bf16[576,128]{1,0:T(8,128)(2,1)S(1)}, u32[]{:S(2)}, u32[]{:S(2)}) collective-permute-start(bf16[576,128]{1,0:T(8,128)(2,1)} %get-tuple-element.151), channel_id=1, source_target_pairs={{0,6},{1,7},{2,0},{3,1},{4,2},{5,3},{6,4},{7,5},{8,14},{9,15},{10,... | collective-permute-start | bytes 442376 | tf_op jit(solution)/shard_map/ppermute | solution.py:939
  208.9 34.7 %collective-permute-start.46 = (bf16[4,4,256,384]{3,2,1,0:T(8,128)(2,1)}, bf16[4,4,256,384]{3,2,1,0:T(8,128)(2,1)S(1)}, u32[]{:S(2)}, u32[]{:S(2)}) collective-permute-start(bf16[4,4,256,384]{3,2,1,0:T(8,128)(2,1)} %get-tuple-element.183), channel_id=1, source_target_pairs={{0,1},{1,0},{2,3},{3,2},{4,5},{5,4},{6,7},{7,6},{8,9},{9,8},{10,11... | collective-permute-start | bytes 9437192 | tf_op jit(solution)/shard_map/ppermute | solution.py:845
  240.1 21.2 %collective-permute-start.59 = (bf16[4,160,128]{2,1,0:T(8,128)(2,1)S(1)}, bf16[4,160,128]{2,1,0:T(8,128)(2,1)S(1)}, u32[]{:S(2)}, u32[]{:S(2)}) collective-permute-start(bf16[4,160,128]{2,1,0:T(8,128)(2,1)S(1)} %get-tuple-element.257), channel_id=1, source_target_pairs={{0,24},{8,16},{16,8},{24,0},{1,25},{9,17},{17,9},{25,1},{2,26},{10... | collective-permute-start | bytes 491528 | tf_op jit(solution)/shard_map/ppermute | solution.py:839
  241.1 22.1 %collective-permute-start.58 = (bf16[4,160,128]{2,1,0:T(8,128)(2,1)S(1)}, bf16[4,160,128]{2,1,0:T(8,128)(2,1)S(1)}, u32[]{:S(2)}, u32[]{:S(2)}) collective-permute-start(bf16[4,160,128]{2,1,0:T(8,128)(2,1)S(1)} %get-tuple-element.258), channel_id=1, source_target_pairs={{0,16},{8,24},{16,0},{24,8},{1,17},{9,25},{17,1},{25,9},{2,18},{10... | collective-permute-start | bytes 491528 | tf_op jit(solution)/shard_map/ppermute | solution.py:839
  242.6 22.2 %collective-permute-start.57 = (bf16[4,160,128]{2,1,0:T(8,128)(2,1)S(1)}, bf16[4,160,128]{2,1,0:T(8,128)(2,1)S(1)}, u32[]{:S(2)}, u32[]{:S(2)}) collective-permute-start(bf16[4,160,128]{2,1,0:T(8,128)(2,1)S(1)} %get-tuple-element.259), channel_id=1, source_target_pairs={{0,8},{8,0},{16,24},{24,16},{1,9},{9,1},{17,25},{25,17},{2,10},{10... | collective-permute-start | bytes 491528 | tf_op jit(solution)/shard_map/ppermute | solution.py:839
  244.2 18.1 %collective-permute-start.51 = (bf16[4,112,384]{2,1,0:T(8,128)(2,1)S(1)}, bf16[4,112,384]{2,1,0:T(8,128)(2,1)S(1)}, u32[]{:S(2)}, u32[]{:S(2)}) collective-permute-start(bf16[4,112,384]{2,1,0:T(8,128)(2,1)S(1)} %add_convert_fusion.6), channel_id=1, source_target_pairs={{0,8},{8,0},{16,24},{24,16},{1,9},{9,1},{17,25},{25,17},{2,10},{10... | collective-permute-start | bytes 1032200 | tf_op jit(solution)/shard_map/ppermute | solution.py:854
  245.3 15.0 %collective-permute-start.47 = (bf16[4,144,384]{2,1,0:T(8,128)(2,1)S(1)}, bf16[4,144,384]{2,1,0:T(8,128)(2,1)S(1)}, u32[]{:S(2)}, u32[]{:S(2)}) collective-permute-start(bf16[4,144,384]{2,1,0:T(8,128)(2,1)S(1)} %add_convert_fusion.3), channel_id=1, source_target_pairs={{0,16},{8,24},{16,0},{24,8},{1,17},{9,25},{17,1},{25,9},{2,18},{10... | collective-permute-start | bytes 1327112 | tf_op jit(solution)/shard_map/ppermute | solution.py:853
  260.3 10.9 %collective-permute-start.50 = (bf16[4,112,384]{2,1,0:T(8,128)(2,1)S(1)}, bf16[4,112,384]{2,1,0:T(8,128)(2,1)S(1)}, u32[]{:S(2)}, u32[]{:S(2)}) collective-permute-start(bf16[4,112,384]{2,1,0:T(8,128)(2,1)S(1)} %add_convert_fusion.7), channel_id=1, source_target_pairs={{0,8},{8,0},{16,24},{24,16},{1,9},{9,1},{17,25},{25,17},{2,10},{10... | collective-permute-start | bytes 1032200 | tf_op jit(solution)/shard_map/ppermute | solution.py:855
  261.3 13.1 %collective-permute-start.49 = (bf16[4,144,384]{2,1,0:T(8,128)(2,1)S(1)}, bf16[4,144,384]{2,1,0:T(8,128)(2,1)S(1)}, u32[]{:S(2)}, u32[]{:S(2)}) collective-permute-start(bf16[4,144,384]{2,1,0:T(8,128)(2,1)S(1)} %add_convert_fusion.1), channel_id=1, source_target_pairs={{0,16},{8,24},{16,0},{24,8},{1,17},{9,25},{17,1},{25,9},{2,18},{10... | collective-permute-start | bytes 1327112 | tf_op jit(solution)/shard_map/ppermute | solution.py:856
  262.3 17.7 %collective-permute-start.48 = (bf16[4,144,384]{2,1,0:T(8,128)(2,1)S(1)}, bf16[4,144,384]{2,1,0:T(8,128)(2,1)S(1)}, u32[]{:S(2)}, u32[]{:S(2)}) collective-permute-start(bf16[4,144,384]{2,1,0:T(8,128)(2,1)S(1)} %add_convert_fusion.2), channel_id=1, source_target_pairs={{0,8},{8,0},{16,24},{24,16},{1,9},{9,1},{17,25},{25,17},{2,10},{10... | collective-permute-start | bytes 1327112 | tf_op jit(solution)/shard_map/ppermute | solution.py:858
  263.2 16.9 %collective-permute-start.52 = (bf16[4,112,384]{2,1,0:T(8,128)(2,1)S(1)}, bf16[4,112,384]{2,1,0:T(8,128)(2,1)S(1)}, u32[]{:S(2)}, u32[]{:S(2)}) collective-permute-start(bf16[4,112,384]{2,1,0:T(8,128)(2,1)S(1)} %add_convert_fusion.5), channel_id=1, source_target_pairs={{0,16},{8,24},{16,0},{24,8},{1,17},{9,25},{17,1},{25,9},{2,18},{10... | collective-permute-start | bytes 1032200 | tf_op jit(solution)/shard_map/ppermute | solution.py:859
  264.9 17.0 %collective-permute-start.35 = (bf16[576,128]{1,0:T(8,128)(2,1)S(1)}, bf16[576,128]{1,0:T(8,128)(2,1)S(1)}, u32[]{:S(2)}, u32[]{:S(2)}) collective-permute-start(bf16[576,128]{1,0:T(8,128)(2,1)S(1)} %copy-done.58), channel_id=1, source_target_pairs={{0,2},{1,3},{2,4},{3,5},{4,6},{5,7},{6,0},{7,1},{8,10},{9,11},{10,... | collective-permute-start | bytes 442376 | tf_op jit(solution)/shard_map/ppermute | solution.py:939
  271.2 14.0 %collective-permute-start.36 = (bf16[576,128]{1,0:T(8,128)(2,1)S(1)}, bf16[576,128]{1,0:T(8,128)(2,1)S(1)}, u32[]{:S(2)}, u32[]{:S(2)}) collective-permute-start(bf16[576,128]{1,0:T(8,128)(2,1)S(1)} %copy-done.57), channel_id=1, source_target_pairs={{0,4},{1,5},{2,6},{3,7},{4,0},{5,1},{6,2},{7,3},{8,12},{9,13},{10,... | collective-permute-start | bytes 442376 | tf_op jit(solution)/shard_map/ppermute | solution.py:939
  274.4 11.4 %collective-permute-start.37 = (bf16[576,128]{1,0:T(8,128)(2,1)S(1)}, bf16[576,128]{1,0:T(8,128)(2,1)S(1)}, u32[]{:S(2)}, u32[]{:S(2)}) collective-permute-start(bf16[576,128]{1,0:T(8,128)(2,1)S(1)} %copy-done.56), channel_id=1, source_target_pairs={{0,6},{1,7},{2,0},{3,1},{4,2},{5,3},{6,4},{7,5},{8,14},{9,15},{10,... | collective-permute-start | bytes 442376 | tf_op jit(solution)/shard_map/ppermute | solution.py:939
  280.1 12.4 %collective-permute-start.44 = (bf16[576,128]{1,0:T(8,128)(2,1)S(1)}, bf16[576,128]{1,0:T(8,128)(2,1)S(1)}, u32[]{:S(2)}, u32[]{:S(2)}) collective-permute-start(bf16[576,128]{1,0:T(8,128)(2,1)S(1)} %copy-done.60), channel_id=1, source_target_pairs={{0,4},{1,5},{2,6},{3,7},{4,0},{5,1},{6,2},{7,3},{8,12},{9,13},{10,... | collective-permute-start | bytes 442376 | tf_op jit(solution)/shard_map/ppermute | solution.py:939
  281.9 19.0 %collective-permute-start.45 = (bf16[576,128]{1,0:T(8,128)(2,1)S(1)}, bf16[576,128]{1,0:T(8,128)(2,1)S(1)}, u32[]{:S(2)}, u32[]{:S(2)}) collective-permute-start(bf16[576,128]{1,0:T(8,128)(2,1)S(1)} %copy-done.59), channel_id=1, source_target_pairs={{0,6},{1,7},{2,0},{3,1},{4,2},{5,3},{6,4},{7,5},{8,14},{9,15},{10,... | collective-permute-start | bytes 442376 | tf_op jit(solution)/shard_map/ppermute | solution.py:939
  285.2 34.3 %collective-permute-start.56 = (bf16[256,384]{1,0:T(8,128)(2,1)S(1)}, bf16[256,384]{1,0:T(8,128)(2,1)S(1)}, u32[]{:S(2)}, u32[]{:S(2)}) collective-permute-start(bf16[256,384]{1,0:T(8,128)(2,1)S(1)} %get-tuple-element.253), channel_id=1, source_target_pairs={{0,6},{1,7},{2,0},{3,1},{4,2},{5,3},{6,4},{7,5},{8,14},{9,15},{10,... | collective-permute-start | bytes 589832 | tf_op jit(solution)/shard_map/ppermute | solution.py:832
  285.8 33.7 %collective-permute-start.54 = (bf16[256,384]{1,0:T(8,128)(2,1)S(1)}, bf16[256,384]{1,0:T(8,128)(2,1)S(1)}, u32[]{:S(2)}, u32[]{:S(2)}) collective-permute-start(bf16[256,384]{1,0:T(8,128)(2,1)S(1)} %get-tuple-element.255), channel_id=1, source_target_pairs={{0,2},{1,3},{2,4},{3,5},{4,6},{5,7},{6,0},{7,1},{8,10},{9,11},{10,... | collective-permute-start | bytes 589832 | tf_op jit(solution)/shard_map/ppermute | solution.py:832
  288.6 30.9 %collective-permute-start.55 = (bf16[256,384]{1,0:T(8,128)(2,1)S(1)}, bf16[256,384]{1,0:T(8,128)(2,1)S(1)}, u32[]{:S(2)}, u32[]{:S(2)}) collective-permute-start(bf16[256,384]{1,0:T(8,128)(2,1)S(1)} %get-tuple-element.256), channel_id=1, source_target_pairs={{0,4},{1,5},{2,6},{3,7},{4,0},{5,1},{6,2},{7,3},{8,12},{9,13},{10,... | collective-permute-start | bytes 589832 | tf_op jit(solution)/shard_map/ppermute | solution.py:832
  292.5 10.1 %collective-permute-start.62 = (bf16[160,128]{1,0:T(8,128)(2,1)S(1)}, bf16[160,128]{1,0:T(8,128)(2,1)S(1)}, u32[]{:S(2)}, u32[]{:S(2)}) collective-permute-start(bf16[160,128]{1,0:T(8,128)(2,1)S(1)} %get-tuple-element.260), channel_id=1, source_target_pairs={{0,6},{1,7},{2,0},{3,1},{4,2},{5,3},{6,4},{7,5},{8,14},{9,15},{10,... | collective-permute-start | bytes 122888 | tf_op jit(solution)/shard_map/ppermute | solution.py:832
  300.9 18.6 %collective-permute-start.61 = (bf16[160,128]{1,0:T(8,128)(2,1)S(1)}, bf16[160,128]{1,0:T(8,128)(2,1)S(1)}, u32[]{:S(2)}, u32[]{:S(2)}) collective-permute-start(bf16[160,128]{1,0:T(8,128)(2,1)S(1)} %get-tuple-element.261), channel_id=1, source_target_pairs={{0,4},{1,5},{2,6},{3,7},{4,0},{5,1},{6,2},{7,3},{8,12},{9,13},{10,... | collective-permute-start | bytes 122888 | tf_op jit(solution)/shard_map/ppermute | solution.py:832
  302.6 16.9 %collective-permute-start.60 = (bf16[160,128]{1,0:T(8,128)(2,1)S(1)}, bf16[160,128]{1,0:T(8,128)(2,1)S(1)}, u32[]{:S(2)}, u32[]{:S(2)}) collective-permute-start(bf16[160,128]{1,0:T(8,128)(2,1)S(1)} %get-tuple-element.262), channel_id=1, source_target_pairs={{0,2},{1,3},{2,4},{3,5},{4,6},{5,7},{6,0},{7,1},{8,10},{9,11},{10,... | collective-permute-start | bytes 122888 | tf_op jit(solution)/shard_map/ppermute | solution.py:832
  (77 other events, 858.2 us)
